TPU v7x, 32 devices: a whole 2x2x4 slice. The times are simulated.
32 devices in a mesh: grp: 2 (over y), gx: 16 (over z, x, core).
Axes of the slice: x: 2, y: 2, z: 4, core: 2. Of those that a mesh axis runs over, the one named last changes fastest.
Arguments:
- activations: bfloat16 [4, 32, 64, 4, 1024], P('grp', None, 'gx'), parts along dimension 0, may hold values from -6 to 6
- cotangent: bfloat16 [4, 32, 64, 4, 1024], P('grp', None, 'gx'), parts along dimension 0, may hold values from -6 to 6
- kernel: bfloat16 [32, 32, 3, 3, 3], replicated, may hold values from -0.21875 to 0.21875
- channel_bias: float32 [32], replicated, may hold values from -3 to 3
Outputs:
- activated: bfloat16 [4, 32, 64, 4, 1024], P('grp', None, 'gx'), parts along dimension 0
- grad_input: bfloat16 [4, 32, 64, 4, 1024], P('grp', None, 'gx'), parts along dimension 0
- grad_kernel: float32 [64, 32, 3, 3, 3], P('grp'), parts along dimension 0
- grad_bias: float32 [64], P('grp'), parts along dimension 0
There are 2 independent parts, one for each index of `grp`. A program takes and returns all parts, laid end to end along the dimension named above; an argument that names none is the same for every part. Nothing has to cross between parts.
All inputs are finite; a program needn't handle non-finite values.
Results may differ from a plain program's by a relative error of at most 0.0055.
Values may be sent and summed in bfloat16 or wider, within the bound.
A program may use at most 256 MiB of HBM per device.

v0:
```python
import jax
import jax.numpy as jnp
from jax import lax
from jax.sharding import PartitionSpec as P


def extended(block, sides, width):
    for axis, dim in sides:
        count = lax.axis_size(axis)
        forward = [(i, i + 1) for i in range(count - 1)]
        backward = [(target, source) for source, target in forward]
        low = lax.ppermute(
            lax.slice_in_dim(block, block.shape[dim] - width, None, axis=dim), axis, forward
        )
        high = lax.ppermute(lax.slice_in_dim(block, 0, width, axis=dim), axis, backward)
        block = jnp.concatenate([low, block, high], axis=dim)
    return block


def convolve(source, filters):
    return lax.conv_general_dilated(
        source,
        filters,
        (1, 1, 1),
        ((0, 0), (1, 1), (1, 1)),
        dimension_numbers=("NCDHW", "OIDHW", "NCDHW"),
        preferred_element_type=jnp.float32,
    )


def kernel_terms(padded, delta):
    result = lax.conv_general_dilated(
        padded,
        delta,
        (1, 1, 1),
        ((0, 0), (1, 1), (1, 1)),
        dimension_numbers=("CNDHW", "IODHW", "NCDHW"),
        preferred_element_type=jnp.float32,
    )
    return jnp.transpose(result, (1, 0, 2, 3, 4))


def gelu_parts(before):
    cumulative = 0.5 * (1.0 + lax.erf(before * 0.7071067811865476))
    density = jnp.exp(-0.5 * before * before) * 0.3989422804014327
    return (before * cumulative, cumulative + before * density)


def per_device(activations, cotangent, kernel, channel_bias):
    offset_term = channel_bias[None, :, None, None, None]
    flipped = jnp.transpose(kernel[:, :, ::-1, ::-1, ::-1], (1, 0, 2, 3, 4))
    padded = extended(activations, (("gx", 2),), 1)
    before = convolve(padded, kernel) + offset_term
    activated_full, derivative = gelu_parts(before)
    activated = activated_full.astype(jnp.bfloat16)
    delta = (cotangent.astype(jnp.float32) * derivative).astype(jnp.bfloat16)
    delta_wide = extended(delta, (("gx", 2),), 1)
    cells = delta.shape[0] * delta.shape[2] * delta.shape[3] * delta.shape[4] * lax.axis_size("gx")
    normalizer = float(cells) ** (-0.5)
    local_kernel = kernel_terms(padded, delta)
    local_bias = jnp.sum(delta.astype(jnp.float32), axis=(0, 2, 3, 4))
    reduced = lax.psum((local_kernel, local_bias), "gx")
    grad_input = convolve(delta_wide, flipped).astype(jnp.bfloat16)
    return (activated, grad_input, reduced[0] * normalizer, reduced[1] * normalizer)


def solution(mesh):
    placed = (P("grp", None, "gx", None, None), P("grp", None, "gx", None, None), P(), P())
    return jax.shard_map(
        per_device,
        mesh=mesh,
        in_specs=placed,
        out_specs=(
            P("grp", None, "gx", None, None),
            P("grp", None, "gx", None, None),
            P("grp", None, None, None, None),
            P("grp"),
        ),
        check_vma=False,
    )
```

profile of v0, /device:TPU:0, one launch (start us, length us, event | category | flops | bytes accessed | tf_op | source)
XLA Modules:
  0.0 629.8 jit_solution(11847770512799942277)
XLA Ops:
  7.2 0.0 copy-start
  7.2 0.0 all-reduce.2.cloned.1.call-start
  7.2 1.8 fusion.32
  9.0 0.2 copy.86
  9.2 2.4 collective-permute-start
  11.6 1.0 copy.87
  12.5 1.3 collective-permute-start.1
  13.8 20.9 %copy.70 = bf16[2,32,4,4,1024]{1,0,4,3,2:T(2,128)(2,1)} copy(bf16[2,32,4,4,1024]{4,3,2,1,0:T(4,128)(2,1)} %param.4) | data formatting | bytes 4194304 | tf_op args[0]
  34.7 1.5 copy.69
  36.2 3.7 copy.71
  39.9 24.6 %fusion.38 = bf16[32,6,4,2,1024]{0,3,4,2,1:T(2,128)(2,1)S(1)} fusion(bf16[2,32,1,4,1024]{1,0,4,3,2:T(2,128)(2,1)} %copy.71, bf16[2,32,4,4,1024]{1,0,4,3,2:T(2,128)(2,1)} %copy.70, bf16[2,32,1,4,1024]{1,0,4,3,2:T(2,128)(2,1)S(1)} %copy.69), kind=kLoop, calls=%fused_computation.45 | loop fusion | flops 3145728 | bytes 6291456 | tf_op jit(solution)/shard_map/concatenate | solution.py:16
  64.5 25.3 %fusion.45 = bf16[2,32,6,4,1024]{1,0,4,3,2:T(2,128)(2,1)} fusion(bf16[2,32,1,4,1024]{1,0,4,3,2:T(2,128)(2,1)S(1)} %copy-done.3, bf16[2,32,4,4,1024]{1,0,4,3,2:T(2,128)(2,1)} %copy.70, bf16[2,32,1,4,1024]{1,0,4,3,2:T(2,128)(2,1)S(1)} %copy.69), kind=kLoop, calls=%bitcast_fusion.clone.1 | loop fusion | flops 3145728 | bytes 6291456 | tf_op jit(solution)/shard_map/transpose | solution.py:40
  89.8 13.8 %pad = bf16[32,6,4,2,1032]{0,3,4,2,1:T(2,128)(2,1)S(1)} pad(bf16[32,6,4,2,1024]{0,3,4,2,1:T(2,128)(2,1)S(1)} %fusion.38, bf16[]{:T(256)} %constant.17), padding=0_0x0_0x0_0x0_0x1_7 | pad | bytes 6316034 | tf_op jit(solution)/shard_map/concatenate | solution.py:16
  103.6 4.7 copy.73
  108.4 0.1 slice.21
  108.4 29.4 %fusion.4 = f32[4,4,16,129,32]{4,2,3,1,0:T(8,128)} fusion(bf16[32,32,3,3,3]{1,0,4,3,2:T(8,128)(2,1)S(1)} %copy-done, bf16[32,6,4,2,7,2]{0,4,3,5,2,1:T(8,128)(2,1)S(1)} %slice.21, bf16[32,6,4,2,8,129]{0,4,3,5,2,1:T(8,128)(2,1)S(1)} %copy.73), kind=kOutput, calls=%fused_computation.5 | convolution fusion | flops 1531404288 | bytes 7495680 | tf_op jit(solution)/shard_map/conv_general_dilated | solution.py:21
  137.9 18.0 %copy.74 = f32[4,4,16,129,32]{3,4,2,1,0:T(8,128)} copy(f32[4,4,16,129,32]{4,2,3,1,0:T(8,128)} %fusion.4) | data formatting | bytes 8454144 | tf_op jit(solution)/shard_map/conv_general_dilated | solution.py:21
  155.9 8.5 %fusion.19 = (f32[4,4,16,129,32]{3,4,2,1,0:T(8,128)S(1)}, bf16[4,4,16,129,32]{3,4,2,1,0:T(8,128)(2,1)}) fusion(f32[4,4,16,129,32]{3,4,2,1,0:T(8,128)} %copy.74, f32[32]{0:T(128)S(1)} %copy-done.6, pred[16,129]{1,0:T(8,128)(4,1)S(1)} %copy-done.4), kind=kLoop, calls=%fused_computation.20 | loop fusion | flops 12681216 | bytes 10569872 | tf_op jit(solution)/shard_map/add | solution.py:46
  164.3 9.7 %copy.77 = f32[4,4,16,129,32]{3,2,4,1,0:T(8,128)} copy(f32[4,4,16,129,32]{3,4,2,1,0:T(8,128)S(1)} %get-tuple-element.26) | data formatting | bytes 8454144 | tf_op jit(solution)/shard_map/add | solution.py:46
  174.0 10.3 %reshape.24 = f32[4,4,2,1032,32]{3,2,4,1,0:T(2,128)} reshape(f32[4,4,16,129,32]{3,2,4,1,0:T(8,128)} %copy.77) | data formatting | bytes 8454144 | tf_op jit(solution)/shard_map/add | solution.py:46
  184.3 7.4 %convert_reduce_fusion = (f32[32]{0:T(128)}, bf16[2,32,4,4,1024]{4,0,1,3,2:T(2,128)(2,1)S(1)}) fusion(f32[4,4,2,1032,32]{3,2,4,1,0:T(2,128)} %reshape.24, bf16[2,32,4,4,1024]{4,3,2,1,0:T(4,128)(2,1)} %param.5), kind=kLoop, calls=%fused_computation.30 | loop fusion | flops 5242848 | bytes 8388736 | tf_op jit(solution)/shard_map/reduce_sum | solution.py:61
  191.8 1.7 fusion.31
  193.4 14.6 %copy.82 = bf16[2,32,4,4,1024]{1,0,4,3,2:T(2,128)(2,1)} copy(bf16[2,32,4,4,1024]{4,0,1,3,2:T(2,128)(2,1)S(1)} %get-tuple-element.25) | data formatting | bytes 4194304 | tf_op jit(solution)/shard_map/convert_element_type | solution.py:56
  208.0 5.9 collective-permute-start.2
  213.9 1.3 collective-permute-start.3
  215.2 7.0 %copy.75 = bf16[4,4,16,129,32]{3,2,4,1,0:T(8,128)(2,1)} copy(bf16[4,4,16,129,32]{3,4,2,1,0:T(8,128)(2,1)} %get-tuple-element.27) | data formatting | bytes 4227072 | tf_op jit(solution)/shard_map/convert_element_type | solution.py:55
  222.2 9.5 %reshape.15 = bf16[4,4,2,1032,32]{3,2,4,1,0:T(2,128)(2,1)} reshape(bf16[4,4,16,129,32]{3,2,4,1,0:T(8,128)(2,1)} %copy.75) | data formatting | bytes 4227072 | tf_op jit(solution)/shard_map/convert_element_type | solution.py:55
  231.7 176.7 %fusion.33 = f32[32,32,3,3,3]{0,1,4,3,2:T(8,128)} fusion(bf16[2,32,4,4,1024]{1,0,4,3,2:T(2,128)(2,1)} %copy.82, bf16[2,32,6,4,1024]{1,0,4,3,2:T(2,128)(2,1)} %fusion.45), kind=kOutput, calls=%fused_computation.44 | convolution fusion | flops 1508966400 | bytes 5353472 | tf_op jit(solution)/shard_map/transpose | solution.py:40
  408.4 4.6 slice_bitcast_fusion.2
  413.0 0.0 all-reduce.2.cloned.1.call-update
  413.0 35.1 %psum.15 = f32[32]{0:T(128)S(1)} all-reduce(f32[32]{0:T(128)S(1)} %copy-done.7), channel_id=1, replica_groups=mesh['grp'=2,'gx'=16] {'gx'}, use_global_device_ids=true, to_apply=%region_2.0 | all-reduce | flops 32 | bytes 256 | tf_op jit(solution)/shard_map/psum | solution.py:62
  448.1 0.5 broadcast_multiply_fusion.1
  448.6 4.5 copy.83
  453.2 54.3 %all-reduce.2.cloned.1.call-done = f32[32,32,3,3,3]{0,1,4,3,2:T(8,128)} async-done(((f32[32,32,3,3,3]{0,1,4,3,2:T(8,128)}), f32[32,32,3,3,3]{0,1,4,3,2:T(8,128)}) %all-reduce.2.cloned.1.call-update) | async-done | bytes 110608 | tf_op jit(solution)/shard_map/psum | solution.py:62
  507.4 1.1 broadcast_multiply_fusion
  508.5 0.9 copy.85
  509.4 6.3 maximum_bitcast_fusion
  515.7 7.7 %pad.2 = bf16[32,6,4,2,1032]{4,3,0,2,1:T(2,128)(2,1)} pad(bf16[32,6,4,2,1024]{4,3,0,2,1:T(2,128)(2,1)S(1)} %maximum_bitcast_fusion, bf16[]{:T(256)} %constant.17), padding=0_0x0_0x0_0x0_0x1_7 | pad | bytes 6316034 | tf_op jit(solution)/shard_map/concatenate | solution.py:16
  523.4 13.6 %reshape.18 = bf16[32,6,4,2,8,129]{5,4,3,0,2,1:T(8,128)(2,1)} reshape(bf16[32,6,4,2,1032]{4,3,0,2,1:T(2,128)(2,1)} %pad.2) | data formatting | bytes 6340608 | tf_op jit(solution)/shard_map/conv_general_dilated | solution.py:21
  537.0 20.1 %copy.79 = bf16[32,6,4,2,8,129]{0,4,3,5,2,1:T(8,128)(2,1)} copy(bf16[32,6,4,2,8,129]{5,4,3,0,2,1:T(8,128)(2,1)} %reshape.18) | data formatting | bytes 6340608 | tf_op jit(solution)/shard_map/conv_general_dilated | solution.py:21
  557.1 1.0 slice.26
  558.1 28.8 %fusion.8 = bf16[4,4,16,129,32]{4,2,3,1,0:T(8,128)(2,1)} fusion(bf16[32,32,3,3,3]{1,0,4,3,2:T(8,128)(2,1)S(1)} %copy-done, bf16[32,6,4,2,7,2]{0,4,3,5,2,1:T(8,128)(2,1)S(1)} %slice.26, bf16[32,6,4,2,8,129]{0,4,3,5,2,1:T(8,128)(2,1)} %copy.79), kind=kOutput, calls=%fused_computation.8 | convolution fusion | flops 1531404288 | bytes 5382144 | tf_op jit(solution)/shard_map/conv_general_dilated | solution.py:21
  586.9 14.4 %copy.80 = bf16[4,4,16,129,32]{3,4,2,1,0:T(8,128)(2,1)} copy(bf16[4,4,16,129,32]{4,2,3,1,0:T(8,128)(2,1)} %fusion.8) | data formatting | bytes 4227072 | tf_op jit(solution)/shard_map/conv_general_dilated | solution.py:21
  601.3 3.3 select_convert_fusion
  604.6 4.8 copy.81
  609.4 8.8 %reshape.22 = bf16[4,4,2,1032,32]{3,2,4,1,0:T(2,128)(2,1)S(1)} reshape(bf16[4,4,16,129,32]{3,2,4,1,0:T(8,128)(2,1)} %copy.81) | data formatting | bytes 4227072 | tf_op jit(solution)/shard_map/convert_element_type | solution.py:63
  618.2 1.5 slice_bitcast_fusion.1
  619.8 2.9 copy.84
  (19 shorter events, 0.0 us)
Async XLA Ops:
  7.2 101.3 %copy-start = (bf16[32,32,3,3,3]{1,0,4,3,2:T(8,128)(2,1)S(1)}, bf16[32,32,3,3,3]{1,0,4,3,2:T(8,128)(2,1)}, u32[]{:S(2)}) copy-start(bf16[32,32,3,3,3]{1,0,4,3,2:T(8,128)(2,1)} %param.6) | copy-start | bytes 165892
  7.2 500.2 %all-reduce.2.cloned.1.call-start = ((), (), s32[]{:S(2)}) async-start(), calls=%async_computation | async-start | bytes 884736 | tf_op jit(solution)/shard_map/psum | solution.py:62
  9.2 25.6 %collective-permute-start = (bf16[2,32,1,4,1024]{4,1,3,2,0:T(8,128)(2,1)S(1)}, bf16[2,32,1,4,1024]{4,1,3,2,0:T(8,128)(2,1)S(1)}, u32[]{:S(2)}, u32[]{:S(2)}) collective-permute-start(bf16[2,32,1,4,1024]{4,1,3,2,0:T(8,128)(2,1)S(1)} %copy.86), channel_id=1, source_target_pairs={{0,1},{1,2},{2,3},{3,4},{4,5},{5,6},{6,7},{7,8},{8,9},{9,10},{10,1... | collective-permute-start | bytes 1572872 | tf_op jit(solution)/shard_map/ppermute | solution.py:12
  12.5 23.6 %collective-permute-start.1 = (bf16[2,32,1,4,1024]{4,1,3,2,0:T(8,128)(2,1)}, bf16[2,32,1,4,1024]{4,1,3,2,0:T(8,128)(2,1)S(1)}, u32[]{:S(2)}, u32[]{:S(2)}) collective-permute-start(bf16[2,32,1,4,1024]{4,1,3,2,0:T(8,128)(2,1)} %copy.87), channel_id=1, source_target_pairs={{1,0},{2,1},{3,2},{4,3},{5,4},{6,5},{7,6},{8,7},{9,8},{10,9},{11,1... | collective-permute-start | bytes 1572872 | tf_op jit(solution)/shard_map/ppermute | solution.py:15
  39.9 24.6 %copy-start.3 = (bf16[2,32,1,4,1024]{1,0,4,3,2:T(2,128)(2,1)S(1)}, bf16[2,32,1,4,1024]{1,0,4,3,2:T(2,128)(2,1)}, u32[]{:S(2)}) copy-start(bf16[2,32,1,4,1024]{1,0,4,3,2:T(2,128)(2,1)} %copy.71) | copy-start | bytes 1572868
  137.9 18.0 %copy-start.4 = (pred[16,129]{1,0:T(8,128)(4,1)S(1)}, pred[16,129]{1,0:T(8,128)(4,1)}, u32[]{:S(2)}) copy-start(pred[16,129]{1,0:T(8,128)(4,1)} %constant.25) | copy-start | bytes 6196
  137.9 18.0 %copy-start.6 = (f32[32]{0:T(128)S(1)}, f32[32]{0:T(128)}, u32[]{:S(2)}) copy-start(f32[32]{0:T(128)} %param.7) | copy-start | bytes 388
  191.8 30.5 %copy-start.1 = (bf16[2,32,4,4,1024]{4,0,1,3,2:T(2,128)(2,1)}, bf16[2,32,4,4,1024]{4,0,1,3,2:T(2,128)(2,1)S(1)}, u32[]{:S(2)}) copy-start(bf16[2,32,4,4,1024]{4,0,1,3,2:T(2,128)(2,1)S(1)} %get-tuple-element.25) | copy-start | bytes 6291460
  208.0 301.4 %collective-permute-start.2 = (bf16[2,32,1,4,1024]{4,0,1,3,2:T(2,128)(2,1)}, bf16[2,32,1,4,1024]{4,0,1,3,2:T(2,128)(2,1)}, u32[]{:S(2)}, u32[]{:S(2)}) collective-permute-start(bf16[2,32,1,4,1024]{4,0,1,3,2:T(2,128)(2,1)} %get-tuple-element.28), channel_id=1, source_target_pairs={{0,1},{1,2},{2,3},{3,4},{4,5},{5,6},{6,7},{7,8},{8,9},{9,10},{10,1... | collective-permute-start | bytes 1572872 | tf_op jit(solution)/shard_map/ppermute | solution.py:12
  213.9 295.5 %collective-permute-start.3 = (bf16[2,32,1,4,1024]{4,0,1,3,2:T(2,128)(2,1)}, bf16[2,32,1,4,1024]{4,0,1,3,2:T(2,128)(2,1)}, u32[]{:S(2)}, u32[]{:S(2)}) collective-permute-start(bf16[2,32,1,4,1024]{4,0,1,3,2:T(2,128)(2,1)} %get-tuple-element.29), channel_id=1, source_target_pairs={{1,0},{2,1},{3,2},{4,3},{5,4},{6,5},{7,6},{8,7},{9,8},{10,9},{11,1... | collective-permute-start | bytes 1572872 | tf_op jit(solution)/shard_map/ppermute | solution.py:15
  231.7 181.3 %copy-start.7 = (f32[32]{0:T(128)S(1)}, f32[32]{0:T(128)}, u32[]{:S(2)}) copy-start(f32[32]{0:T(128)} %get-tuple-element.24) | copy-start | bytes 388
  408.4 101.1 %copy-start.2 = (bf16[2,32,4,4,1024]{4,0,1,3,2:T(2,128)(2,1)S(1)}, bf16[2,32,4,4,1024]{4,0,1,3,2:T(2,128)(2,1)}, u32[]{:S(2)}) copy-start(bf16[2,32,4,4,1024]{4,0,1,3,2:T(2,128)(2,1)} %copy-done.1) | copy-start | bytes 6291460
  586.9 14.4 %copy-start.5 = (pred[16,129]{1,0:T(8,128)(4,1)S(1)}, pred[16,129]{1,0:T(8,128)(4,1)}, u32[]{:S(2)}) copy-start(pred[16,129]{1,0:T(8,128)(4,1)} %constant.25) | copy-start | bytes 6196
Sparse Core Ops, SparseCore 0:
  413.1 94.2 all-reduce.1
where the time goes:
time: 637 us; the launch traced here: 630 us
  matrix products  235 us (37%)
  local copies, waits for them, and re-layouts  203 us (32%)
  other arithmetic  76.9 us (12%)
  waiting for transfers between devices  54.3 us (9%)
  blocking collectives  35.1 us (6%)
  between operations  14.5 us (2%)
  starting transfers between devices  10.9 us (2%)
    transpose x1, matrix products, kernel_terms(): return jnp.transpose(result, (1, 0, 2, 3, 4))  177 us
    conv_general_dilated x7, local copies, waits for them, and re-layouts, convolve(): lax.conv_general_dilated(source, filters, (1, 1, 1), ((0, 0), (1, 1), (1,...  71.8 us
    conv_general_dilated x2, matrix products, convolve(): lax.conv_general_dilated(source, filters, (1, 1, 1), ((0, 0), (1, 1), (1,...  58.2 us
    psum x1, waiting for transfers between devices, per_device(): reduced = lax.psum((local_kernel, local_bias), 'gx')  54.3 us
    psum x1, blocking collectives, per_device(): reduced = lax.psum((local_kernel, local_bias), 'gx')  35.1 us
    concatenate x2, other arithmetic, extended(): block = jnp.concatenate([low, block, high], axis=dim)  30.9 us
    unnamed x22, local copies, waits for them, and re-layouts  30.5 us
    transpose x1, other arithmetic, kernel_terms(): return jnp.transpose(result, (1, 0, 2, 3, 4))  25.3 us
  transfers between devices with their start and end apart: 5, of which 1 were waited for; matrix products, arithmetic and copies ran while one was open for 36% of the time, Pallas kernels for 0%

commit v1 on v0

v1 whole, which is shorter than its diff:
```python
import functools

import jax
import jax.numpy as jnp
from jax import lax
from jax.experimental import pallas as pl
from jax.experimental.pallas import tpu as pltpu
from jax.sharding import PartitionSpec as P

F32 = jnp.float32
BF16 = jnp.bfloat16


def one_hot_rows(rows, group, dtype):
    r = lax.broadcasted_iota(jnp.int32, (rows, rows // group), 0)
    c = lax.broadcasted_iota(jnp.int32, (rows, rows // group), 1)
    return jnp.where(r // group == c, 1.0, 0.0).astype(dtype)


def one_hot_cols(rows, group, dtype):
    r = lax.broadcasted_iota(jnp.int32, (rows // group, rows), 0)
    c = lax.broadcasted_iota(jnp.int32, (rows // group, rows), 1)
    return jnp.where(c // group == r, 1.0, 0.0).astype(dtype)


def band(rows, yb):
    r = lax.broadcasted_iota(jnp.int32, (rows, rows), 0)
    c = lax.broadcasted_iota(jnp.int32, (rows, rows), 1)
    return c % yb - r % yb


def build_weights(taps_ref, w_ref, rows, yb, backward):
    spread_rows = one_hot_rows(rows, yb, BF16)
    spread_cols = one_hot_cols(rows, yb, BF16)
    offset = band(rows, yb)
    w_ref[...] = jnp.zeros_like(w_ref)
    for i in range(3):
        for k in range(3):
            block = jnp.zeros((rows, rows), F32)
            for j in range(3):
                tap = taps_ref[(i * 3 + j) * 3 + k]
                wide = jnp.dot(tap, spread_cols, preferred_element_type=F32).astype(BF16)
                full = jnp.dot(spread_rows, wide, preferred_element_type=F32)
                want = (1 - j) if backward else (j - 1)
                block = block + jnp.where(offset == want, full, 0.0)
            block = block.astype(BF16)
            for xo in range(2):
                xi = xo - i + 2 if backward else xo + i
                w_ref[k, xo * rows:(xo + 1) * rows, xi * rows:(xi + 1) * rows] = block


def shifted(v):
    zero = jnp.zeros((v.shape[0], 1), v.dtype)
    return (
        jnp.concatenate([zero, v[:, :-1]], axis=1),
        jnp.concatenate([v[:, 1:], zero], axis=1),
    )


def forward_kernel(act_ref, lo_ref, hi_ref, cot_ref, taps_ref, bias_ref,
                   activated_ref, delta_ref, planes_ref, w_ref, s_ref):
    _, c, nx, yb, z = act_ref.shape
    rows = c * yb

    @pl.when(pl.program_id(0) == 0)
    def _():
        build_weights(taps_ref, w_ref, rows, yb, False)

    for p in range(nx + 2):
        if p == 0:
            v = lo_ref[0, :, 0]
        elif p == nx + 1:
            v = hi_ref[0, :, 0]
        else:
            v = act_ref[0, :, p - 1]
        v = v.reshape(rows, z)
        planes_ref[0, p] = v
        before, after = shifted(v)
        at = slice(p * rows, (p + 1) * rows)
        s_ref[0, at] = before
        s_ref[1, at] = v
        s_ref[2, at] = after
    zc = 256
    for q in range(nx // 2):
        at = slice(2 * q * rows, (2 * q + 4) * rows)
        for n in range(z // zc):
            zs = slice(n * zc, (n + 1) * zc)
            pre = jnp.dot(w_ref[0], s_ref[0, at, zs], preferred_element_type=F32)
            pre += jnp.dot(w_ref[1], s_ref[1, at, zs], preferred_element_type=F32)
            pre += jnp.dot(w_ref[2], s_ref[2, at, zs], preferred_element_type=F32)
            for xo in range(2):
                x = 2 * q + xo
                t = pre[xo * rows:(xo + 1) * rows] + bias_ref[:, 0:1]
                cumulative = 0.5 * (1.0 + lax.erf(t * 0.7071067811865476))
                density = jnp.exp(-0.5 * t * t) * 0.3989422804014327
                activated_ref[0, :, x, :, zs] = (t * cumulative).astype(BF16).reshape(c, yb, zc)
                g = cot_ref[0, :, x, :, zs].reshape(rows, zc).astype(F32)
                delta_ref[0, x, :, zs] = (g * (cumulative + t * density)).astype(BF16)


def weight_grad_kernel(planes_ref, delta_ref, out_ref, acc_ref, d_ref, bias_ref, *, yb):
    _, nx, rows, z = delta_ref.shape
    step = pl.program_id(0)

    @pl.when(step == 0)
    def _():
        acc_ref[...] = jnp.zeros_like(acc_ref)
        bias_ref[...] = jnp.zeros_like(bias_ref)

    nt = (((1,), (1,)), ((), ()))
    for q in range(nx // 2):
        for xo in range(2):
            v = delta_ref[0, 2 * q + xo]
            before, after = shifted(v)
            for k, part in enumerate((after, v, before)):
                d_ref[(k * 2 + xo) * rows:(k * 2 + xo + 1) * rows] = part
            bias_ref[...] += lax.dot_general(jnp.ones((8, z), BF16), v, nt, preferred_element_type=F32)
        a = planes_ref[0, 2 * q:2 * q + 4].reshape(4 * rows, z)
        acc_ref[...] += lax.dot_general(d_ref[...], a, nt, preferred_element_type=F32)

    @pl.when(step == pl.num_programs(0) - 1)
    def _():
        gather_rows = one_hot_cols(rows, yb, F32)
        gather_cols = one_hot_rows(rows, yb, F32)
        offset = band(rows, yb)
        exact = dict(preferred_element_type=F32, precision=lax.Precision.HIGHEST)
        for i in range(3):
            for k in range(3):
                t = jnp.zeros((rows, rows), F32)
                for xo in range(2):
                    r0 = (k * 2 + xo) * rows
                    c0 = (xo + i) * rows
                    t = t + acc_ref[r0:r0 + rows, c0:c0 + rows]
                for j in range(3):
                    masked = jnp.where(offset == j - 1, t, 0.0)
                    half = jnp.dot(masked, gather_cols, **exact)
                    out_ref[(i * 3 + j) * 3 + k] = jnp.dot(gather_rows, half, **exact)
        c = out_ref.shape[1]
        total = jnp.dot(bias_ref[...], gather_cols, **exact)
        out_ref[27] = jnp.broadcast_to(total[0:1], (c, c))


def input_grad_kernel(delta_ref, lo_ref, hi_ref, taps_ref, out_ref, w_ref, s_ref):
    _, nx, rows, z = delta_ref.shape
    _, c, _, yb, _ = out_ref.shape

    @pl.when(pl.program_id(0) == 0)
    def _():
        build_weights(taps_ref, w_ref, rows, yb, True)

    for p in range(nx + 2):
        if p == 0:
            v = lo_ref[0, 0]
        elif p == nx + 1:
            v = hi_ref[0, 0]
        else:
            v = delta_ref[0, p - 1]
        before, after = shifted(v)
        at = slice(p * rows, (p + 1) * rows)
        s_ref[0, at] = after
        s_ref[1, at] = v
        s_ref[2, at] = before
    zc = 256
    for q in range(nx // 2):
        at = slice(2 * q * rows, (2 * q + 4) * rows)
        for n in range(z // zc):
            zs = slice(n * zc, (n + 1) * zc)
            g = jnp.dot(w_ref[0], s_ref[0, at, zs], preferred_element_type=F32)
            g += jnp.dot(w_ref[1], s_ref[1, at, zs], preferred_element_type=F32)
            g += jnp.dot(w_ref[2], s_ref[2, at, zs], preferred_element_type=F32)
            for xo in range(2):
                part = g[xo * rows:(xo + 1) * rows].astype(BF16)
                out_ref[0, :, 2 * q + xo, :, zs] = part.reshape(c, yb, zc)


def native(c, nx, yb, z):
    return pl.BlockSpec((1, c, nx, yb, z), lambda b: (b, 0, 0, 0, 0))


def plain(nx, rows, z):
    return pl.BlockSpec((1, nx, rows, z), lambda b: (b, 0, 0, 0))


def whole(*shape):
    return pl.BlockSpec(shape, lambda b: (0,) * len(shape))


PARAMS = dict(vmem_limit_bytes=60 * 1024 * 1024, dimension_semantics=("arbitrary",))


def forward(activations, lo, hi, cotangent, taps, bias):
    nb, c, nx, yb, z = activations.shape
    rows = c * yb
    return pl.pallas_call(
        forward_kernel,
        grid=(nb,),
        in_specs=[native(c, nx, yb, z), native(c, 1, yb, z), native(c, 1, yb, z), native(c, nx, yb, z),
                  whole(27, c, c), whole(rows, 128)],
        out_specs=[native(c, nx, yb, z), plain(nx, rows, z), plain(nx + 2, rows, z)],
        out_shape=[jax.ShapeDtypeStruct((nb, c, nx, yb, z), BF16),
                   jax.ShapeDtypeStruct((nb, nx, rows, z), BF16),
                   jax.ShapeDtypeStruct((nb, nx + 2, rows, z), BF16)],
        scratch_shapes=[pltpu.VMEM((3, 2 * rows, 4 * rows), BF16),
                        pltpu.VMEM((3, (nx + 2) * rows, z), BF16)],
        compiler_params=pltpu.CompilerParams(**PARAMS),
        cost_estimate=pl.CostEstimate(flops=nb * nx * 3 * 256 * 512 * z, bytes_accessed=10 << 20, transcendentals=0),
        name="forward",
    )(activations, lo, hi, cotangent, taps, bias)


def weight_grad(planes, delta, c):
    nb, nx, rows, z = delta.shape
    yb = rows // c
    return pl.pallas_call(
        functools.partial(weight_grad_kernel, yb=yb),
        grid=(nb,),
        in_specs=[plain(nx + 2, rows, z), plain(nx, rows, z)],
        out_specs=whole(28, c, c),
        out_shape=jax.ShapeDtypeStruct((28, c, c), F32),
        scratch_shapes=[pltpu.VMEM((6 * rows, 4 * rows), F32),
                        pltpu.VMEM((6 * rows, z), BF16),
                        pltpu.VMEM((8, rows), F32)],
        compiler_params=pltpu.CompilerParams(**PARAMS),
        cost_estimate=pl.CostEstimate(flops=nb * nx * 3 * 256 * 512 * z, bytes_accessed=10 << 20, transcendentals=0),
        name="weight_grad",
    )(planes, delta)


def input_grad(delta, lo, hi, taps, c):
    nb, nx, rows, z = delta.shape
    yb = rows // c
    return pl.pallas_call(
        input_grad_kernel,
        grid=(nb,),
        in_specs=[plain(nx, rows, z), plain(1, rows, z), plain(1, rows, z), whole(27, c, c)],
        out_specs=native(c, nx, yb, z),
        out_shape=jax.ShapeDtypeStruct((nb, c, nx, yb, z), BF16),
        scratch_shapes=[pltpu.VMEM((3, 2 * rows, 4 * rows), BF16),
                        pltpu.VMEM((3, (nx + 2) * rows, z), BF16)],
        compiler_params=pltpu.CompilerParams(**PARAMS),
        cost_estimate=pl.CostEstimate(flops=nb * nx * 3 * 256 * 512 * z, bytes_accessed=10 << 20, transcendentals=0),
        name="input_grad",
    )(delta, lo, hi, taps)


def faces(block, dim):
    count = lax.axis_size("gx")
    up = [(i, i + 1) for i in range(count - 1)]
    down = [(t, s) for s, t in up]
    n = block.shape[dim]
    lo = lax.ppermute(lax.slice_in_dim(block, n - 1, n, axis=dim), "gx", up)
    hi = lax.ppermute(lax.slice_in_dim(block, 0, 1, axis=dim), "gx", down)
    return lo, hi


def per_device(activations, cotangent, kernel, channel_bias):
    nb, c, nx, yb, z = activations.shape
    rows = c * yb
    taps = jnp.transpose(kernel, (2, 3, 4, 0, 1)).reshape(27, c, c)
    taps_back = jnp.transpose(kernel, (2, 3, 4, 1, 0)).reshape(27, c, c)
    bias = jnp.broadcast_to(jnp.repeat(channel_bias, yb)[:, None], (rows, 128))
    lo, hi = faces(activations, 2)
    activated, delta, planes = forward(activations, lo, hi, cotangent, taps, bias)
    dlo, dhi = faces(delta, 1)
    sums = weight_grad(planes, delta, c)
    cells = nb * nx * yb * z * lax.axis_size("gx")
    reduced = lax.psum(sums, "gx") * (float(cells) ** -0.5)
    grad_input = input_grad(delta, dlo, dhi, taps_back, c)
    grad_kernel = jnp.transpose(reduced[:27].reshape(3, 3, 3, c, c), (3, 4, 0, 1, 2))
    return activated, grad_input, grad_kernel, reduced[27, 0]


def solution(mesh):
    placed = (P("grp", None, "gx", None, None), P("grp", None, "gx", None, None), P(), P())
    return jax.shard_map(
        per_device,
        mesh=mesh,
        in_specs=placed,
        out_specs=(
            P("grp", None, "gx", None, None),
            P("grp", None, "gx", None, None),
            P("grp", None, None, None, None),
            P("grp"),
        ),
        check_vma=False,
    )
```

time: 637 us -> 163 us (0.26); the launches traced: 630 us -> 163 us
  matrix products: 235 us -> 0 us
  local copies, waits for them, and re-layouts: 203 us -> 5.91 us
  other arithmetic: 76.9 us -> 1.06 us
  waiting for transfers between devices: 54.3 us -> 90.7 us
  blocking collectives: 35.1 us -> 0 us
  Pallas kernels: 0 us -> 30.6 us
  starting transfers between devices: 10.9 us -> 20.2 us
    transpose x1 -> x0, matrix products: 177 us -> none  [kernel_terms(): return jnp.transpose(result, (1, 0, 2, 3, 4))]
    conv_general_dilated x7 -> x0, local copies, waits for them, and re-layouts: 71.8 us -> none  [convolve(): lax.conv_general_dilated(source, filters, (1, 1, 1), ((0, 0), (1, 1), (1,...]
    conv_general_dilated x2 -> x0, matrix products: 58.2 us -> none  [convolve(): lax.conv_general_dilated(source, filters, (1, 1, 1), ((0, 0), (1, 1), (1,...]
    convert_element_type x7 -> x0, local copies, waits for them, and re-layouts: 50.8 us -> none  [the longest x3 21.1 us: per_device(): activated = activated_full.astype(jnp.bfloat16)]
    psum x1, waiting for transfers between devices: 54.3 us -> 89.4 us  [per_device(): reduced = lax.psum(sums, 'gx') * float(cells) ** (-0.5)]
    psum x1 -> x0, blocking collectives: 35.1 us -> none  [per_device(): reduced = lax.psum((local_kernel, local_bias), 'gx')]
    concatenate x2 -> x0, other arithmetic: 30.9 us -> none  [extended(): block = jnp.concatenate([low, block, high], axis=dim)]
    pallas_call x0 -> x3, Pallas kernels: none -> 30.6 us  [the longest x1 11.9 us: forward(): pl.pallas_call(forward_kernel, grid=(nb,), in_specs=[native(c, nx, yb, z)...]
  transfers between devices with their start and end apart: 5 -> 5, of which waited for: 1 -> 2; matrix products, arithmetic and copies ran while one was open for 36% -> 2% of each run, Pallas kernels for 0% -> 0%
where the time goes in v1:
time: 163 us
  waiting for transfers between devices  90.7 us (56%)
  Pallas kernels  30.6 us (19%)
  starting transfers between devices  20.2 us (12%)
  between operations  14.1 us (9%)
  local copies, waits for them, and re-layouts  5.91 us (4%)
    psum x1, waiting for transfers between devices, per_device(): reduced = lax.psum(sums, 'gx') * float(cells) ** (-0.5)  89.4 us
    ppermute x2, starting transfers between devices, faces(): lo = lax.ppermute(lax.slice_in_dim(block, n - 1, n, axis=dim), 'gx', up)  17.6 us
    pallas_call x1, Pallas kernels, forward(): pl.pallas_call(forward_kernel, grid=(nb,), in_specs=[native(c, nx, yb, z)...  11.9 us
    pallas_call x1, Pallas kernels, weight_grad(): pl.pallas_call(functools.partial(weight_grad_kernel, yb=yb), grid=(nb,),...  10.4 us
    pallas_call x1, Pallas kernels, input_grad(): pl.pallas_call(input_grad_kernel, grid=(nb,), in_specs=[plain(nx, rows, z...  8.26 us
  transfers between devices with their start and end apart: 5, of which 2 were waited for; matrix products, arithmetic and copies ran while one was open for 2% of the time, Pallas kernels for 0%

profile of v1, /device:TPU:0, one launch (start us, length us, event | category | flops | bytes accessed | tf_op | source)
XLA Modules:
  0.0 162.6 jit_solution(3956231803645669021)
XLA Ops:
  7.2 0.0 copy-start.2
  7.2 0.0 all-reduce.2.cloned.1.call-start
  7.2 1.7 %fusion.1 = (bf16[2,32,1,4,1024]{4,3,2,1,0:T(4,128)(2,1)S(1)}, bf16[2,32,1,4,1024]{4,3,2,1,0:T(4,128)(2,1)S(1)}) fusion(bf16[2,32,4,4,1024]{4,3,2,1,0:T(4,128)(2,1)} %act_ref.1), kind=kLoop, calls=%fused_computation.3 | loop fusion | bytes 2097152 | tf_op jit(solution)/shard_map/slice | solution.py:252
  8.9 1.3 collective-permute-start.1
  10.2 3.1 %collective-permute-start = (bf16[2,32,1,4,1024]{4,3,2,1,0:T(4,128)(2,1)S(1)}, bf16[2,32,1,4,1024]{4,3,2,1,0:T(4,128)(2,1)S(1)}, u32[]{:S(2)}, u32[]{:S(2)}) collective-permute-start(bf16[2,32,1,4,1024]{4,3,2,1,0:T(4,128)(2,1)S(1)} %get-tuple-element.13), channel_id=1, source_target_pairs={{0,1},{1,2},{2,3},{3,4},{4,5},{5,6},{6,7},{7,8},{8,9},{9,10},{10,1... | collective-permute-start | bytes 1572872 | tf_op jit(solution)/shard_map/ppermute | solution.py:251
  13.3 0.0 copy-done.2
  13.3 0.1 broadcast_in_dim.10
  13.4 0.1 broadcast_in_dim.11
  13.5 0.0 collective-permute-done.1.hi_ref
  13.5 0.0 copy-start.4
  13.5 1.3 collective-permute-done.lo_ref
  14.8 0.0 copy-start.6
  14.8 0.8 broadcast_in_dim.12.bias_ref
  15.6 0.0 copy-done.4
  15.6 0.0 copy-done.6
  15.6 11.9 %forward.1 = (bf16[2,32,4,4,1024]{4,3,2,1,0:T(4,128)(2,1)}, bf16[2,4,128,1024]{3,2,1,0:T(8,128)(2,1)}, bf16[2,6,128,1024]{3,2,1,0:T(8,128)(2,1)}) custom-call(bf16[2,32,4,4,1024]{4,3,2,1,0:T(4,128)(2,1)} %act_ref.1, bf16[2,32,1,4,1024]{4,3,2,1,0:T(4,128)(2,1)} %copy-done.6, bf16[2,32,1,4,1024]{4,3,2,1,0:T(4,128)(2,1)} %copy-done.4, ...), custom_call_target="tpu_custom_call" | custom-call | flops 3221225472 | bytes 10485760 | tf_op jit(solution)/shard_map/forward/pallas_call | solution.py:194
  27.6 0.0 copy-start
  27.6 10.4 %weight_grad.1 = f32[28,32,32]{2,1,0:T(8,128)} custom-call(bf16[2,6,128,1024]{3,2,1,0:T(8,128)(2,1)} %get-tuple-element.9.planes_ref, bf16[2,4,128,1024]{3,2,1,0:T(8,128)(2,1)} %get-tuple-element.8.delta_ref), custom_call_target="tpu_custom_call" | custom-call | flops 3221225472 | bytes 10485760 | tf_op jit(solution)/shard_map/weight_grad/pallas_call | solution.py:214
  38.0 0.0 copy-start.1
  38.0 0.0 all-reduce.2.cloned.1.call-update
  38.0 0.0 copy-done
  38.0 0.1 fusion
  38.1 1.3 collective-permute-start.3
  39.4 14.5 %collective-permute-start.2 = (bf16[2,1,128,1024]{3,2,1,0:T(8,128)(2,1)S(1)}, bf16[2,1,128,1024]{3,2,1,0:T(8,128)(2,1)S(1)}, u32[]{:S(2)}, u32[]{:S(2)}) collective-permute-start(bf16[2,1,128,1024]{3,2,1,0:T(8,128)(2,1)S(1)} %get-tuple-element.11), channel_id=1, source_target_pairs={{0,1},{1,2},{2,3},{3,4},{4,5},{5,6},{6,7},{7,8},{8,9},{9,10},{10,1... | collective-permute-start | bytes 1572872 | tf_op jit(solution)/shard_map/ppermute | solution.py:251
  53.9 0.0 copy-done.1
  53.9 0.8 copy.9
  54.8 89.4 %all-reduce.2.cloned.1.call-done = f32[28,32,32]{2,1,0:T(8,128)} async-done(((f32[28,32,32]{2,1,0:T(8,128)}), f32[28,32,32]{2,1,0:T(8,128)}) %all-reduce.2.cloned.1.call-update) | async-done | bytes 114704 | tf_op jit(solution)/shard_map/psum | solution.py:267
  144.1 1.1 broadcast_multiply_fusion
  145.2 0.8 slice.24
  146.0 0.5 slice_bitcast_fusion
  146.5 0.0 collective-permute-done.3.hi_ref
  146.5 0.0 copy-start.3
  146.5 0.0 collective-permute-done.2.lo_ref
  146.5 0.0 copy-start.5
  146.5 0.8 copy-done.3
  147.3 0.2 copy-done.5
  147.5 8.3 %input_grad.1 = bf16[2,32,4,4,1024]{4,3,2,1,0:T(4,128)(2,1)} custom-call(bf16[2,4,128,1024]{3,2,1,0:T(8,128)(2,1)} %get-tuple-element.8.delta_ref, bf16[2,1,128,1024]{3,2,1,0:T(8,128)(2,1)} %copy-done.5, bf16[2,1,128,1024]{3,2,1,0:T(8,128)(2,1)} %copy-done.3, bf16[27,32,32]{2,1,0:T(8,128)(2,1)} %bitcast.13), custom_call_target="tpu_custom_call" | custom-call | flops 3221225472 | bytes 10485760 | tf_op jit(solution)/shard_map/input_grad/pallas_call | solution.py:232
Async XLA Ops:
  7.2 6.1 %copy-start.2 = (f32[32]{0:T(128)S(1)}, f32[32]{0:T(128)}, u32[]{:S(2)}) copy-start(f32[32]{0:T(128)} %param.7) | copy-start | bytes 388
  7.2 136.9 %all-reduce.2.cloned.1.call-start = ((), (), s32[]{:S(2)}) async-start(), calls=%async_computation | async-start | bytes 917504 | tf_op jit(solution)/shard_map/psum | solution.py:267
  8.9 4.6 %collective-permute-start.1 = (bf16[2,32,1,4,1024]{4,3,2,1,0:T(4,128)(2,1)S(1)}, bf16[2,32,1,4,1024]{4,3,2,1,0:T(4,128)(2,1)S(1)}, u32[]{:S(2)}, u32[]{:S(2)}) collective-permute-start(bf16[2,32,1,4,1024]{4,3,2,1,0:T(4,128)(2,1)S(1)} %get-tuple-element.12), channel_id=1, source_target_pairs={{1,0},{2,1},{3,2},{4,3},{5,4},{6,5},{7,6},{8,7},{9,8},{10,9},{11,1... | collective-permute-start | bytes 1572872 | tf_op jit(solution)/shard_map/ppermute | solution.py:252
  10.2 4.6 %collective-permute-start = (bf16[2,32,1,4,1024]{4,3,2,1,0:T(4,128)(2,1)S(1)}, bf16[2,32,1,4,1024]{4,3,2,1,0:T(4,128)(2,1)S(1)}, u32[]{:S(2)}, u32[]{:S(2)}) collective-permute-start(bf16[2,32,1,4,1024]{4,3,2,1,0:T(4,128)(2,1)S(1)} %get-tuple-element.13), channel_id=1, source_target_pairs={{0,1},{1,2},{2,3},{3,4},{4,5},{5,6},{6,7},{7,8},{8,9},{9,10},{10,1... | collective-permute-start | bytes 1572872 | tf_op jit(solution)/shard_map/ppermute | solution.py:251
  13.5 2.1 %copy-start.4 = (bf16[2,32,1,4,1024]{4,3,2,1,0:T(4,128)(2,1)}, bf16[2,32,1,4,1024]{4,3,2,1,0:T(4,128)(2,1)S(1)}, u32[]{:S(2)}) copy-start(bf16[2,32,1,4,1024]{4,3,2,1,0:T(4,128)(2,1)S(1)} %collective-permute-done.1.hi_ref) | copy-start | bytes 1572868
  14.8 0.8 copy-start.6
  27.6 10.4 %copy-start = (bf16[2,4,128,1024]{3,2,1,0:T(8,128)(2,1)S(1)}, bf16[2,4,128,1024]{3,2,1,0:T(8,128)(2,1)}, u32[]{:S(2)}) copy-start(bf16[2,4,128,1024]{3,2,1,0:T(8,128)(2,1)} %get-tuple-element.8.delta_ref) | copy-start | bytes 6291460
  38.0 15.9 %copy-start.1 = (bf16[32,32,3,3,3]{1,0,4,3,2:T(8,128)(2,1)S(1)}, bf16[32,32,3,3,3]{1,0,4,3,2:T(8,128)(2,1)}, u32[]{:S(2)}) copy-start(bf16[32,32,3,3,3]{1,0,4,3,2:T(8,128)(2,1)} %param.6) | copy-start | bytes 165892
  38.1 108.4 %collective-permute-start.3 = (bf16[2,1,128,1024]{3,2,1,0:T(8,128)(2,1)S(1)}, bf16[2,1,128,1024]{3,2,1,0:T(8,128)(2,1)S(1)}, u32[]{:S(2)}, u32[]{:S(2)}) collective-permute-start(bf16[2,1,128,1024]{3,2,1,0:T(8,128)(2,1)S(1)} %get-tuple-element.10), channel_id=1, source_target_pairs={{1,0},{2,1},{3,2},{4,3},{5,4},{6,5},{7,6},{8,7},{9,8},{10,9},{11,1... | collective-permute-start | bytes 1572872 | tf_op jit(solution)/shard_map/ppermute | solution.py:252
  39.4 107.1 %collective-permute-start.2 = (bf16[2,1,128,1024]{3,2,1,0:T(8,128)(2,1)S(1)}, bf16[2,1,128,1024]{3,2,1,0:T(8,128)(2,1)S(1)}, u32[]{:S(2)}, u32[]{:S(2)}) collective-permute-start(bf16[2,1,128,1024]{3,2,1,0:T(8,128)(2,1)S(1)} %get-tuple-element.11), channel_id=1, source_target_pairs={{0,1},{1,2},{2,3},{3,4},{4,5},{5,6},{6,7},{7,8},{8,9},{9,10},{10,1... | collective-permute-start | bytes 1572872 | tf_op jit(solution)/shard_map/ppermute | solution.py:251
  146.5 0.8 copy-start.3
  146.5 1.0 copy-start.5
Sparse Core Ops, SparseCore 0:
  38.1 105.9 all-reduce.1

commit v2 on v1

--- a/solution.py
+++ b/solution.py
@@ -120,6 +120,13 @@
 
     @pl.when(step == pl.num_programs(0) - 1)
     def _():
+        c = rows // yb
+        out_ref[...] = jnp.zeros_like(out_ref)
+
+        def put(tap, value):
+            row, col = tap // 4 * c, tap % 4 * c
+            out_ref[row:row + c, col:col + c] = value
+
         gather_rows = one_hot_cols(rows, yb, F32)
         gather_cols = one_hot_rows(rows, yb, F32)
         offset = band(rows, yb)
@@ -134,10 +141,9 @@
                 for j in range(3):
                     masked = jnp.where(offset == j - 1, t, 0.0)
                     half = jnp.dot(masked, gather_cols, **exact)
-                    out_ref[(i * 3 + j) * 3 + k] = jnp.dot(gather_rows, half, **exact)
-        c = out_ref.shape[1]
+                    put((i * 3 + j) * 3 + k, jnp.dot(gather_rows, half, **exact))
         total = jnp.dot(bias_ref[...], gather_cols, **exact)
-        out_ref[27] = jnp.broadcast_to(total[0:1], (c, c))
+        put(27, jnp.broadcast_to(total[0:1], (c, c)))
 
 
 def input_grad_kernel(delta_ref, lo_ref, hi_ref, taps_ref, out_ref, w_ref, s_ref):
@@ -208,15 +214,75 @@
     )(activations, lo, hi, cotangent, taps, bias)
 
 
-def weight_grad(planes, delta, c):
+def all_sum_kernel(x_ref, out_ref, recv, mine, gathered, send1, recv1, send2, recv2, *, n, scale):
+    me = lax.axis_index("gx")
+    c = out_ref.shape[1]
+
+    def scatter(d, owner):
+        return pltpu.make_async_remote_copy(
+            src_ref=x_ref.at[owner], dst_ref=recv.at[d - 1], send_sem=send1.at[d - 1], recv_sem=recv1.at[d - 1],
+            device_id={"gx": owner}, device_id_type=pl.DeviceIdType.MESH)
+
+    def spread(d, slot, peer):
+        return pltpu.make_async_remote_copy(
+            src_ref=mine, dst_ref=gathered.at[slot], send_sem=send2.at[d - 1], recv_sem=recv2.at[d - 1],
+            device_id={"gx": peer}, device_id_type=pl.DeviceIdType.MESH)
+
+    def each(f):
+        def step(d, carry):
+            f(d, lax.rem(me + d, n), lax.rem(me + n - d, n))
+            return carry
+        lax.fori_loop(1, n, step, 0)
+
+    barrier = pltpu.get_barrier_semaphore()
+    each(lambda d, to, source: pl.semaphore_signal(
+        barrier, inc=1, device_id={"gx": to}, device_id_type=pl.DeviceIdType.MESH))
+    pl.semaphore_wait(barrier, n - 1)
+    each(lambda d, to, source: scatter(d, to).start())
+    each(lambda d, to, source: scatter(d, to).wait_recv())
+    total = (x_ref[me] + jnp.sum(recv[...], axis=0)) * scale
+    mine[...] = total
+    gathered[me] = total
+    each(lambda d, to, source: spread(d, me, to).start())
+    each(lambda d, to, source: spread(d, source, to).wait_recv())
+    flat = gathered[...].reshape(-1, 128)
+    for tap in range(28):
+        row, col = tap // 4 * c, tap % 4 * c
+        out_ref[tap] = flat[row:row + c, col:col + c]
+    each(lambda d, to, source: scatter(d, to).wait_send())
+    each(lambda d, to, source: spread(d, me, to).wait_send())
+
+
+def chunk_rows(c, n):
+    rows = 28 * c * c // 128
+    return -(-rows // (8 * n)) * 8
+
+
+def all_sum(sums, c, n, scale):
+    r = chunk_rows(c, n)
+    vmem = pl.BlockSpec(memory_space=pltpu.VMEM)
+    return pl.pallas_call(
+        functools.partial(all_sum_kernel, n=n, scale=scale),
+        in_specs=[vmem],
+        out_specs=vmem,
+        out_shape=jax.ShapeDtypeStruct((28, c, c), F32),
+        scratch_shapes=[pltpu.VMEM((n - 1, r, 128), F32), pltpu.VMEM((r, 128), F32), pltpu.VMEM((n, r, 128), F32)]
+        + [pltpu.SemaphoreType.DMA((n - 1,))] * 4,
+        compiler_params=pltpu.CompilerParams(collective_id=0, has_side_effects=True),
+        cost_estimate=pl.CostEstimate(flops=1 << 20, bytes_accessed=16 << 20, transcendentals=0),
+        name="all_sum",
+    )(sums.reshape(n, r, 128))
+
+
+def weight_grad(planes, delta, c, n):
     nb, nx, rows, z = delta.shape
     yb = rows // c
     return pl.pallas_call(
         functools.partial(weight_grad_kernel, yb=yb),
         grid=(nb,),
         in_specs=[plain(nx + 2, rows, z), plain(nx, rows, z)],
-        out_specs=whole(28, c, c),
-        out_shape=jax.ShapeDtypeStruct((28, c, c), F32),
+        out_specs=whole(n * chunk_rows(c, n), 128),
+        out_shape=jax.ShapeDtypeStruct((n * chunk_rows(c, n), 128), F32),
         scratch_shapes=[pltpu.VMEM((6 * rows, 4 * rows), F32),
                         pltpu.VMEM((6 * rows, z), BF16),
                         pltpu.VMEM((8, rows), F32)],
@@ -262,9 +328,10 @@
     lo, hi = faces(activations, 2)
     activated, delta, planes = forward(activations, lo, hi, cotangent, taps, bias)
     dlo, dhi = faces(delta, 1)
-    sums = weight_grad(planes, delta, c)
-    cells = nb * nx * yb * z * lax.axis_size("gx")
-    reduced = lax.psum(sums, "gx") * (float(cells) ** -0.5)
+    n = lax.axis_size("gx")
+    sums = weight_grad(planes, delta, c, n)
+    cells = nb * nx * yb * z * n
+    reduced = all_sum(sums, c, n, float(cells) ** -0.5)
     grad_input = input_grad(delta, dlo, dhi, taps_back, c)
     grad_kernel = jnp.transpose(reduced[:27].reshape(3, 3, 3, c, c), (3, 4, 0, 1, 2))
     return activated, grad_input, grad_kernel, reduced[27, 0]

time: 163 us -> 77.7 us (0.48)
  waiting for transfers between devices: 90.7 us -> 0.45 us
  Pallas kernels: 30.6 us -> 47.2 us
  between operations: 14.1 us -> 0.74 us
  local copies, waits for them, and re-layouts: 5.91 us -> 8.85 us
    psum x1 -> x0, waiting for transfers between devices: 89.4 us -> none  [per_device(): reduced = lax.psum(sums, 'gx') * float(cells) ** (-0.5)]
    pallas_call x0 -> x1, Pallas kernels: none -> 17.1 us  [all_sum(): pl.pallas_call(functools.partial(all_sum_kernel, n=n, scale=scale), in_sp...]
  transfers between devices with their start and end apart: 5 -> 4, of which waited for: 2 -> 1; matrix products, arithmetic and copies ran while one was open for 2% -> 5% of each run, Pallas kernels for 0% -> 35%
where the time goes in v2:
time: 77.7 us; the launch traced here: 77.4 us
  Pallas kernels  47.2 us (61%)
  starting transfers between devices  20.2 us (26%)
  local copies, waits for them, and re-layouts  8.85 us (11%)
    ppermute x2, starting transfers between devices, faces(): lo = lax.ppermute(lax.slice_in_dim(block, n - 1, n, axis=dim), 'gx', up)  17.6 us
    pallas_call x1, Pallas kernels, all_sum(): pl.pallas_call(functools.partial(all_sum_kernel, n=n, scale=scale), in_sp...  17.1 us
    pallas_call x1, Pallas kernels, forward(): pl.pallas_call(forward_kernel, grid=(nb,), in_specs=[native(c, nx, yb, z)...  12 us
    pallas_call x1, Pallas kernels, weight_grad(): pl.pallas_call(functools.partial(weight_grad_kernel, yb=yb), grid=(nb,),...  9.89 us
    pallas_call x1, Pallas kernels, input_grad(): pl.pallas_call(input_grad_kernel, grid=(nb,), in_specs=[plain(nx, rows, z...  8.27 us
    slice x2, local copies, waits for them, and re-layouts, faces(): hi = lax.ppermute(lax.slice_in_dim(block, 0, 1, axis=dim), 'gx', down)  3.02 us
    ppermute x2, starting transfers between devices, faces(): hi = lax.ppermute(lax.slice_in_dim(block, 0, 1, axis=dim), 'gx', down)  2.58 us
    slice x1, local copies, waits for them, and re-layouts, per_device(): reduced[:27].reshape(3, 3, 3, c, c)  1.8 us
  transfers between devices with their start and end apart: 4, of which 1 were waited for; matrix products, arithmetic and copies ran while one was open for 5% of the time, Pallas kernels for 35%

profile of v2, /device:TPU:0, one launch (start us, length us, event | category | flops | bytes accessed | tf_op | source)
XLA Modules:
  0.0 77.4 jit_solution(7389895520220537331)
XLA Ops:
  0.6 0.0 copy-start.1
  0.6 0.0 copy-start
  0.7 1.7 %fusion.1 = (bf16[2,32,1,4,1024]{4,3,2,1,0:T(4,128)(2,1)S(1)}, bf16[2,32,1,4,1024]{4,3,2,1,0:T(4,128)(2,1)S(1)}) fusion(bf16[2,32,4,4,1024]{4,3,2,1,0:T(4,128)(2,1)} %act_ref.1), kind=kLoop, calls=%fused_computation.2 | loop fusion | bytes 2097152 | tf_op jit(solution)/shard_map/slice | solution.py:318
  2.4 1.3 %collective-permute-start.1 = (bf16[2,32,1,4,1024]{4,3,2,1,0:T(4,128)(2,1)S(1)}, bf16[2,32,1,4,1024]{4,3,2,1,0:T(4,128)(2,1)S(1)}, u32[]{:S(2)}, u32[]{:S(2)}) collective-permute-start(bf16[2,32,1,4,1024]{4,3,2,1,0:T(4,128)(2,1)S(1)} %get-tuple-element.12), channel_id=1, source_target_pairs={{1,0},{2,1},{3,2},{4,3},{5,4},{6,5},{7,6},{8,7},{9,8},{10,9},{11,1... | collective-permute-start | bytes 1572872 | tf_op jit(solution)/shard_map/ppermute | solution.py:318
  3.7 3.1 %collective-permute-start = (bf16[2,32,1,4,1024]{4,3,2,1,0:T(4,128)(2,1)S(1)}, bf16[2,32,1,4,1024]{4,3,2,1,0:T(4,128)(2,1)S(1)}, u32[]{:S(2)}, u32[]{:S(2)}) collective-permute-start(bf16[2,32,1,4,1024]{4,3,2,1,0:T(4,128)(2,1)S(1)} %get-tuple-element.13), channel_id=1, source_target_pairs={{0,1},{1,2},{2,3},{3,4},{4,5},{5,6},{6,7},{7,8},{8,9},{9,10},{10,1... | collective-permute-start | bytes 1572872 | tf_op jit(solution)/shard_map/ppermute | solution.py:317
  6.8 0.0 copy-done.1
  6.8 0.1 broadcast_in_dim.10
  6.9 0.1 broadcast_in_dim.11
  7.0 0.0 copy-done
  7.0 0.8 %copy.9 = bf16[3,3,3,32,32]{4,3,2,1,0:T(8,128)(2,1)} copy(bf16[3,3,3,32,32]{3,4,2,1,0:T(8,128)(2,1)S(1)} %bitcast.13) | data formatting | bytes 110592 | tf_op jit(solution)/shard_map/transpose | solution.py:326
  7.8 0.0 collective-permute-done.1.hi_ref
  7.8 0.0 copy-start.2
  7.8 0.4 collective-permute-done.lo_ref
  8.3 0.0 copy-start.4
  8.3 0.9 %broadcast_in_dim.12.bias_ref = f32[128,128]{1,0:T(8,128)} broadcast(f32[128]{0:T(128)S(1)} %broadcast_in_dim.11), dimensions={0} | broadcast | bytes 66048 | tf_op jit(solution)/shard_map/broadcast_in_dim | solution.py:327
  9.1 0.0 copy-done.2
  9.1 0.0 copy-done.4
  9.1 12.0 %forward.1 = (bf16[2,32,4,4,1024]{4,3,2,1,0:T(4,128)(2,1)}, bf16[2,4,128,1024]{3,2,1,0:T(8,128)(2,1)}, bf16[2,6,128,1024]{3,2,1,0:T(8,128)(2,1)}) custom-call(bf16[2,32,4,4,1024]{4,3,2,1,0:T(4,128)(2,1)} %act_ref.1, bf16[2,32,1,4,1024]{4,3,2,1,0:T(4,128)(2,1)} %copy-done.4, bf16[2,32,1,4,1024]{4,3,2,1,0:T(4,128)(2,1)} %copy-done.2, ...), custom_call_target="tpu_custom_call" | custom-call | flops 3221225472 | bytes 10485760 | tf_op jit(solution)/shard_map/forward/pallas_call | solution.py:200
  21.1 1.3 %fusion = (bf16[2,1,128,1024]{3,2,1,0:T(8,128)(2,1)S(1)}, bf16[2,1,128,1024]{3,2,1,0:T(8,128)(2,1)S(1)}) fusion(bf16[2,4,128,1024]{3,2,1,0:T(8,128)(2,1)} %get-tuple-element.8.delta_ref), kind=kLoop, calls=%fused_computation.1 | loop fusion | bytes 2097152 | tf_op jit(solution)/shard_map/slice | solution.py:318
  22.4 1.3 %collective-permute-start.3 = (bf16[2,1,128,1024]{3,2,1,0:T(8,128)(2,1)S(1)}, bf16[2,1,128,1024]{3,2,1,0:T(8,128)(2,1)S(1)}, u32[]{:S(2)}, u32[]{:S(2)}) collective-permute-start(bf16[2,1,128,1024]{3,2,1,0:T(8,128)(2,1)S(1)} %get-tuple-element.10), channel_id=1, source_target_pairs={{1,0},{2,1},{3,2},{4,3},{5,4},{6,5},{7,6},{8,7},{9,8},{10,9},{11,1... | collective-permute-start | bytes 1572872 | tf_op jit(solution)/shard_map/ppermute | solution.py:318
  23.7 14.5 %collective-permute-start.2 = (bf16[2,1,128,1024]{3,2,1,0:T(8,128)(2,1)S(1)}, bf16[2,1,128,1024]{3,2,1,0:T(8,128)(2,1)S(1)}, u32[]{:S(2)}, u32[]{:S(2)}) collective-permute-start(bf16[2,1,128,1024]{3,2,1,0:T(8,128)(2,1)S(1)} %get-tuple-element.11), channel_id=1, source_target_pairs={{0,1},{1,2},{2,3},{3,4},{4,5},{5,6},{6,7},{7,8},{8,9},{9,10},{10,1... | collective-permute-start | bytes 1572872 | tf_op jit(solution)/shard_map/ppermute | solution.py:317
  38.2 9.9 %weight_grad.1 = f32[256,128]{1,0:T(8,128)} custom-call(bf16[2,6,128,1024]{3,2,1,0:T(8,128)(2,1)} %get-tuple-element.9.planes_ref, bf16[2,4,128,1024]{3,2,1,0:T(8,128)(2,1)} %get-tuple-element.8.delta_ref), custom_call_target="tpu_custom_call" | custom-call | flops 3221225472 | bytes 10485760 | tf_op jit(solution)/shard_map/weight_grad/pallas_call | solution.py:280
  48.1 17.1 %all_sum.1 = f32[28,32,32]{2,1,0:T(8,128)} custom-call(f32[16,16,128]{2,1,0:T(8,128)} %bitcast.15), custom_call_target="tpu_custom_call" | custom-call | flops 1048576 | bytes 16777216 | tf_op jit(solution)/shard_map/all_sum/pallas_call | solution.py:264
  65.1 1.8 %slice.22 = f32[27,32,32]{2,1,0:T(8,128)} slice(f32[28,32,32]{2,1,0:T(8,128)} %all_sum.1), slice={[0:27], [0:32], [0:32]} | slice | bytes 221184 | tf_op jit(solution)/shard_map/slice | solution.py:336
  66.9 1.2 %slice_bitcast_fusion = f32[32]{0:T(128)} fusion(f32[28,32,32]{2,1,0:T(8,128)} %all_sum.1), kind=kLoop, calls=%fused_computation | loop fusion | bytes 256 | tf_op jit(solution)/shard_map/squeeze | solution.py:337
  68.1 0.0 collective-permute-done.3.hi_ref
  68.1 0.0 copy-start.3
  68.1 0.0 collective-permute-done.2.lo_ref
  68.1 0.0 copy-start.5
  68.1 0.8 %copy-done.3 = bf16[2,1,128,1024]{3,2,1,0:T(8,128)(2,1)} copy-done((bf16[2,1,128,1024]{3,2,1,0:T(8,128)(2,1)}, bf16[2,1,128,1024]{3,2,1,0:T(8,128)(2,1)S(1)}, u32[]{:S(2)}) %copy-start.3) | copy-done | bytes 524312
  68.9 0.2 copy-done.5
  69.1 8.3 %input_grad.1 = bf16[2,32,4,4,1024]{4,3,2,1,0:T(4,128)(2,1)} custom-call(bf16[2,4,128,1024]{3,2,1,0:T(8,128)(2,1)} %get-tuple-element.8.delta_ref, bf16[2,1,128,1024]{3,2,1,0:T(8,128)(2,1)} %copy-done.5, bf16[2,1,128,1024]{3,2,1,0:T(8,128)(2,1)} %copy-done.3, bf16[27,32,32]{2,1,0:T(8,128)(2,1)} %bitcast.14), custom_call_target="tpu_custom_call" | custom-call | flops 3221225472 | bytes 10485760 | tf_op jit(solution)/shard_map/input_grad/pallas_call | solution.py:298
Async XLA Ops:
  0.6 6.2 %copy-start.1 = (f32[32]{0:T(128)S(1)}, f32[32]{0:T(128)}, u32[]{:S(2)}) copy-start(f32[32]{0:T(128)} %param.7) | copy-start | bytes 388
  0.6 6.3 %copy-start = (bf16[32,32,3,3,3]{1,0,4,3,2:T(8,128)(2,1)S(1)}, bf16[32,32,3,3,3]{1,0,4,3,2:T(8,128)(2,1)}, u32[]{:S(2)}) copy-start(bf16[32,32,3,3,3]{1,0,4,3,2:T(8,128)(2,1)} %param.6) | copy-start | bytes 165892
  2.4 5.4 %collective-permute-start.1 = (bf16[2,32,1,4,1024]{4,3,2,1,0:T(4,128)(2,1)S(1)}, bf16[2,32,1,4,1024]{4,3,2,1,0:T(4,128)(2,1)S(1)}, u32[]{:S(2)}, u32[]{:S(2)}) collective-permute-start(bf16[2,32,1,4,1024]{4,3,2,1,0:T(4,128)(2,1)S(1)} %get-tuple-element.12), channel_id=1, source_target_pairs={{1,0},{2,1},{3,2},{4,3},{5,4},{6,5},{7,6},{8,7},{9,8},{10,9},{11,1... | collective-permute-start | bytes 1572872 | tf_op jit(solution)/shard_map/ppermute | solution.py:318
  3.7 4.6 %collective-permute-start = (bf16[2,32,1,4,1024]{4,3,2,1,0:T(4,128)(2,1)S(1)}, bf16[2,32,1,4,1024]{4,3,2,1,0:T(4,128)(2,1)S(1)}, u32[]{:S(2)}, u32[]{:S(2)}) collective-permute-start(bf16[2,32,1,4,1024]{4,3,2,1,0:T(4,128)(2,1)S(1)} %get-tuple-element.13), channel_id=1, source_target_pairs={{0,1},{1,2},{2,3},{3,4},{4,5},{5,6},{6,7},{7,8},{8,9},{9,10},{10,1... | collective-permute-start | bytes 1572872 | tf_op jit(solution)/shard_map/ppermute | solution.py:317
  7.8 1.3 %copy-start.2 = (bf16[2,32,1,4,1024]{4,3,2,1,0:T(4,128)(2,1)}, bf16[2,32,1,4,1024]{4,3,2,1,0:T(4,128)(2,1)S(1)}, u32[]{:S(2)}) copy-start(bf16[2,32,1,4,1024]{4,3,2,1,0:T(4,128)(2,1)S(1)} %collective-permute-done.1.hi_ref) | copy-start | bytes 1572868
  8.3 0.9 %copy-start.4 = (bf16[2,32,1,4,1024]{4,3,2,1,0:T(4,128)(2,1)}, bf16[2,32,1,4,1024]{4,3,2,1,0:T(4,128)(2,1)S(1)}, u32[]{:S(2)}) copy-start(bf16[2,32,1,4,1024]{4,3,2,1,0:T(4,128)(2,1)S(1)} %collective-permute-done.lo_ref) | copy-start | bytes 1572868
  22.4 45.7 %collective-permute-start.3 = (bf16[2,1,128,1024]{3,2,1,0:T(8,128)(2,1)S(1)}, bf16[2,1,128,1024]{3,2,1,0:T(8,128)(2,1)S(1)}, u32[]{:S(2)}, u32[]{:S(2)}) collective-permute-start(bf16[2,1,128,1024]{3,2,1,0:T(8,128)(2,1)S(1)} %get-tuple-element.10), channel_id=1, source_target_pairs={{1,0},{2,1},{3,2},{4,3},{5,4},{6,5},{7,6},{8,7},{9,8},{10,9},{11,1... | collective-permute-start | bytes 1572872 | tf_op jit(solution)/shard_map/ppermute | solution.py:318
  23.7 44.4 %collective-permute-start.2 = (bf16[2,1,128,1024]{3,2,1,0:T(8,128)(2,1)S(1)}, bf16[2,1,128,1024]{3,2,1,0:T(8,128)(2,1)S(1)}, u32[]{:S(2)}, u32[]{:S(2)}) collective-permute-start(bf16[2,1,128,1024]{3,2,1,0:T(8,128)(2,1)S(1)} %get-tuple-element.11), channel_id=1, source_target_pairs={{0,1},{1,2},{2,3},{3,4},{4,5},{5,6},{6,7},{7,8},{8,9},{9,10},{10,1... | collective-permute-start | bytes 1572872 | tf_op jit(solution)/shard_map/ppermute | solution.py:317
  68.1 0.8 %copy-start.3 = (bf16[2,1,128,1024]{3,2,1,0:T(8,128)(2,1)}, bf16[2,1,128,1024]{3,2,1,0:T(8,128)(2,1)S(1)}, u32[]{:S(2)}) copy-start(bf16[2,1,128,1024]{3,2,1,0:T(8,128)(2,1)S(1)} %collective-permute-done.3.hi_ref) | copy-start | bytes 1572868
  68.1 1.0 %copy-start.5 = (bf16[2,1,128,1024]{3,2,1,0:T(8,128)(2,1)}, bf16[2,1,128,1024]{3,2,1,0:T(8,128)(2,1)S(1)}, u32[]{:S(2)}) copy-start(bf16[2,1,128,1024]{3,2,1,0:T(8,128)(2,1)S(1)} %collective-permute-done.2.lo_ref) | copy-start | bytes 1572868

commit v3 on v2

--- a/solution.py
+++ b/solution.py
@@ -49,6 +49,14 @@
                 w_ref[k, xo * rows:(xo + 1) * rows, xi * rows:(xi + 1) * rows] = block
 
 
+def weights_kernel(taps_ref, taps_back_ref, bias_ref, w_ref, w_back_ref, column_ref, *, yb):
+    rows = w_ref.shape[1] // 2
+    column = jnp.sum(one_hot_rows(rows, yb, F32) * bias_ref[...], axis=1, keepdims=True)
+    column_ref[...] = jnp.broadcast_to(column, column_ref.shape)
+    build_weights(taps_ref, w_ref, rows, yb, False)
+    build_weights(taps_back_ref, w_back_ref, rows, yb, True)
+
+
 def shifted(v):
     zero = jnp.zeros((v.shape[0], 1), v.dtype)
     return (
@@ -57,15 +65,10 @@
     )
 
 
-def forward_kernel(act_ref, lo_ref, hi_ref, cot_ref, taps_ref, bias_ref,
-                   activated_ref, delta_ref, planes_ref, w_ref, s_ref):
+def forward_kernel(act_ref, lo_ref, hi_ref, cot_ref, w_ref, bias_ref,
+                   activated_ref, delta_ref, planes_ref, s_ref):
     _, c, nx, yb, z = act_ref.shape
     rows = c * yb
-
-    @pl.when(pl.program_id(0) == 0)
-    def _():
-        build_weights(taps_ref, w_ref, rows, yb, False)
-
     for p in range(nx + 2):
         if p == 0:
             v = lo_ref[0, :, 0]
@@ -146,14 +149,9 @@
         put(27, jnp.broadcast_to(total[0:1], (c, c)))
 
 
-def input_grad_kernel(delta_ref, lo_ref, hi_ref, taps_ref, out_ref, w_ref, s_ref):
+def input_grad_kernel(delta_ref, lo_ref, hi_ref, w_ref, out_ref, s_ref):
     _, nx, rows, z = delta_ref.shape
     _, c, _, yb, _ = out_ref.shape
-
-    @pl.when(pl.program_id(0) == 0)
-    def _():
-        build_weights(taps_ref, w_ref, rows, yb, True)
-
     for p in range(nx + 2):
         if p == 0:
             v = lo_ref[0, 0]
@@ -194,27 +192,37 @@
 PARAMS = dict(vmem_limit_bytes=60 * 1024 * 1024, dimension_semantics=("arbitrary",))
 
 
-def forward(activations, lo, hi, cotangent, taps, bias):
+def weights(taps, taps_back, channel_bias, c, yb):
+    rows = c * yb
+    wide = jax.ShapeDtypeStruct((3, 2 * rows, 4 * rows), BF16)
+    return pl.pallas_call(
+        functools.partial(weights_kernel, yb=yb),
+        out_shape=[wide, wide, jax.ShapeDtypeStruct((rows, 128), F32)],
+        cost_estimate=pl.CostEstimate(flops=1 << 30, bytes_accessed=4 << 20, transcendentals=0),
+        name="weights",
+    )(taps, taps_back, channel_bias.reshape(1, c))
+
+
+def forward(activations, lo, hi, cotangent, w, bias):
     nb, c, nx, yb, z = activations.shape
     rows = c * yb
     return pl.pallas_call(
         forward_kernel,
         grid=(nb,),
         in_specs=[native(c, nx, yb, z), native(c, 1, yb, z), native(c, 1, yb, z), native(c, nx, yb, z),
-                  whole(27, c, c), whole(rows, 128)],
+                  whole(3, 2 * rows, 4 * rows), whole(rows, 128)],
         out_specs=[native(c, nx, yb, z), plain(nx, rows, z), plain(nx + 2, rows, z)],
         out_shape=[jax.ShapeDtypeStruct((nb, c, nx, yb, z), BF16),
                    jax.ShapeDtypeStruct((nb, nx, rows, z), BF16),
                    jax.ShapeDtypeStruct((nb, nx + 2, rows, z), BF16)],
-        scratch_shapes=[pltpu.VMEM((3, 2 * rows, 4 * rows), BF16),
-                        pltpu.VMEM((3, (nx + 2) * rows, z), BF16)],
+        scratch_shapes=[pltpu.VMEM((3, (nx + 2) * rows, z), BF16)],
         compiler_params=pltpu.CompilerParams(**PARAMS),
         cost_estimate=pl.CostEstimate(flops=nb * nx * 3 * 256 * 512 * z, bytes_accessed=10 << 20, transcendentals=0),
         name="forward",
-    )(activations, lo, hi, cotangent, taps, bias)
-
-
-def all_sum_kernel(x_ref, out_ref, recv, mine, gathered, send1, recv1, send2, recv2, *, n, scale):
+    )(activations, lo, hi, cotangent, w, bias)
+
+
+def all_sum_kernel(x_ref, out_ref, bias_ref, recv, mine, gathered, send1, recv1, send2, recv2, *, n, scale):
     me = lax.axis_index("gx")
     c = out_ref.shape[1]
 
@@ -246,9 +254,11 @@
     each(lambda d, to, source: spread(d, me, to).start())
     each(lambda d, to, source: spread(d, source, to).wait_recv())
     flat = gathered[...].reshape(-1, 128)
-    for tap in range(28):
+    for tap in range(27):
         row, col = tap // 4 * c, tap % 4 * c
         out_ref[tap] = flat[row:row + c, col:col + c]
+    row, col = 27 // 4 * c, 27 % 4 * c
+    bias_ref[...] = flat[row:row + 1, col:col + c]
     each(lambda d, to, source: scatter(d, to).wait_send())
     each(lambda d, to, source: spread(d, me, to).wait_send())
 
@@ -264,8 +274,8 @@
     return pl.pallas_call(
         functools.partial(all_sum_kernel, n=n, scale=scale),
         in_specs=[vmem],
-        out_specs=vmem,
-        out_shape=jax.ShapeDtypeStruct((28, c, c), F32),
+        out_specs=[vmem, vmem],
+        out_shape=[jax.ShapeDtypeStruct((27, c, c), F32), jax.ShapeDtypeStruct((1, c), F32)],
         scratch_shapes=[pltpu.VMEM((n - 1, r, 128), F32), pltpu.VMEM((r, 128), F32), pltpu.VMEM((n, r, 128), F32)]
         + [pltpu.SemaphoreType.DMA((n - 1,))] * 4,
         compiler_params=pltpu.CompilerParams(collective_id=0, has_side_effects=True),
@@ -292,21 +302,20 @@
     )(planes, delta)
 
 
-def input_grad(delta, lo, hi, taps, c):
+def input_grad(delta, lo, hi, w, c):
     nb, nx, rows, z = delta.shape
     yb = rows // c
     return pl.pallas_call(
         input_grad_kernel,
         grid=(nb,),
-        in_specs=[plain(nx, rows, z), plain(1, rows, z), plain(1, rows, z), whole(27, c, c)],
+        in_specs=[plain(nx, rows, z), plain(1, rows, z), plain(1, rows, z), whole(3, 2 * rows, 4 * rows)],
         out_specs=native(c, nx, yb, z),
         out_shape=jax.ShapeDtypeStruct((nb, c, nx, yb, z), BF16),
-        scratch_shapes=[pltpu.VMEM((3, 2 * rows, 4 * rows), BF16),
-                        pltpu.VMEM((3, (nx + 2) * rows, z), BF16)],
+        scratch_shapes=[pltpu.VMEM((3, (nx + 2) * rows, z), BF16)],
         compiler_params=pltpu.CompilerParams(**PARAMS),
         cost_estimate=pl.CostEstimate(flops=nb * nx * 3 * 256 * 512 * z, bytes_accessed=10 << 20, transcendentals=0),
         name="input_grad",
-    )(delta, lo, hi, taps)
+    )(delta, lo, hi, w)
 
 
 def faces(block, dim):
@@ -321,20 +330,19 @@
 
 def per_device(activations, cotangent, kernel, channel_bias):
     nb, c, nx, yb, z = activations.shape
-    rows = c * yb
     taps = jnp.transpose(kernel, (2, 3, 4, 0, 1)).reshape(27, c, c)
     taps_back = jnp.transpose(kernel, (2, 3, 4, 1, 0)).reshape(27, c, c)
-    bias = jnp.broadcast_to(jnp.repeat(channel_bias, yb)[:, None], (rows, 128))
     lo, hi = faces(activations, 2)
-    activated, delta, planes = forward(activations, lo, hi, cotangent, taps, bias)
+    w, w_back, column = weights(taps, taps_back, channel_bias, c, yb)
+    activated, delta, planes = forward(activations, lo, hi, cotangent, w, column)
     dlo, dhi = faces(delta, 1)
     n = lax.axis_size("gx")
     sums = weight_grad(planes, delta, c, n)
     cells = nb * nx * yb * z * n
-    reduced = all_sum(sums, c, n, float(cells) ** -0.5)
-    grad_input = input_grad(delta, dlo, dhi, taps_back, c)
-    grad_kernel = jnp.transpose(reduced[:27].reshape(3, 3, 3, c, c), (3, 4, 0, 1, 2))
-    return activated, grad_input, grad_kernel, reduced[27, 0]
+    kernel_sums, bias_sums = all_sum(sums, c, n, float(cells) ** -0.5)
+    grad_input = input_grad(delta, dlo, dhi, w_back, c)
+    grad_kernel = jnp.transpose(kernel_sums.reshape(3, 3, 3, c, c), (3, 4, 0, 1, 2))
+    return activated, grad_input, grad_kernel, bias_sums.reshape(c)
 
 
 def solution(mesh):

time: 77.7 us -> 71.9 us (0.925)
  starting transfers between devices: 20.2 us -> 14.4 us
  Pallas kernels: 47.2 us -> 49.4 us
  local copies, waits for them, and re-layouts: 8.85 us -> 7.07 us
    pallas_call x0 -> x1, Pallas kernels: none -> 6.04 us  [weights(): pl.pallas_call(functools.partial(weights_kernel, yb=yb), out_shape=[wide,...]
    ppermute x2, starting transfers between devices: 17.6 us -> 11.8 us  [faces(): lo = lax.ppermute(lax.slice_in_dim(block, n - 1, n, axis=dim), 'gx', up)]
    unnamed x12 -> x16, local copies, waits for them, and re-layouts: 0.97 us -> 3.23 us
    pallas_call x1, Pallas kernels: 12 us -> 9.96 us  [forward(): pl.pallas_call(forward_kernel, grid=(nb,), in_specs=[native(c, nx, yb, z)...]
    pallas_call x1, Pallas kernels: 8.27 us -> 6.35 us  [input_grad(): pl.pallas_call(input_grad_kernel, grid=(nb,), in_specs=[plain(nx, rows, z...]
    slice x1 -> x0, local copies, waits for them, and re-layouts: 1.8 us -> none  [per_device(): reduced[:27].reshape(3, 3, 3, c, c)]
    squeeze x1 -> x0, local copies, waits for them, and re-layouts: 1.17 us -> none  [per_device(): return (activated, grad_input, grad_kernel, reduced[27, 0])]
    broadcast_in_dim x3 -> x0, local copies, waits for them, and re-layouts: 1.04 us -> none  [per_device(): bias = jnp.broadcast_to(jnp.repeat(channel_bias, yb)[:, None], (rows, 128))]
  transfers between devices with their start and end apart: 4 -> 4, of which waited for: 1 -> 0; matrix products, arithmetic and copies ran while one was open for 5% -> 1% of each run, Pallas kernels for 35% -> 46%
where the time goes in v3:
time: 71.9 us; the launch traced here: 71.6 us
  Pallas kernels  49.4 us (69%)
  starting transfers between devices  14.4 us (20%)
  local copies, waits for them, and re-layouts  7.07 us (10%)
  between operations  0.75 us (1%)
    pallas_call x1, Pallas kernels, all_sum(): pl.pallas_call(functools.partial(all_sum_kernel, n=n, scale=scale), in_sp...  17.1 us
    ppermute x2, starting transfers between devices, faces(): lo = lax.ppermute(lax.slice_in_dim(block, n - 1, n, axis=dim), 'gx', up)  11.8 us
    pallas_call x1, Pallas kernels, forward(): pl.pallas_call(forward_kernel, grid=(nb,), in_specs=[native(c, nx, yb, z)...  9.96 us
    pallas_call x1, Pallas kernels, weight_grad(): pl.pallas_call(functools.partial(weight_grad_kernel, yb=yb), grid=(nb,),...  9.89 us
    pallas_call x1, Pallas kernels, input_grad(): pl.pallas_call(input_grad_kernel, grid=(nb,), in_specs=[plain(nx, rows, z...  6.35 us
    pallas_call x1, Pallas kernels, weights(): pl.pallas_call(functools.partial(weights_kernel, yb=yb), out_shape=[wide,...  6.04 us
    unnamed x16, local copies, waits for them, and re-layouts  3.23 us
    slice x2, local copies, waits for them, and re-layouts, faces(): hi = lax.ppermute(lax.slice_in_dim(block, 0, 1, axis=dim), 'gx', down)  3.02 us
  transfers between devices with their start and end apart: 4, of which 0 were waited for; matrix products, arithmetic and copies ran while one was open for 1% of the time, Pallas kernels for 46%

profile of v3, /device:TPU:0, one launch (start us, length us, event | category | flops | bytes accessed | tf_op | source)
XLA Modules:
  0.0 71.6 jit_solution(7056062105853707156)
XLA Ops:
  0.6 0.0 copy-start.1
  0.6 1.7 %fusion.1 = (bf16[2,32,1,4,1024]{4,3,2,1,0:T(4,128)(2,1)S(1)}, bf16[2,32,1,4,1024]{4,3,2,1,0:T(4,128)(2,1)S(1)}) fusion(bf16[2,32,4,4,1024]{4,3,2,1,0:T(4,128)(2,1)} %act_ref.1), kind=kLoop, calls=%fused_computation.1 | loop fusion | bytes 2097152 | tf_op jit(solution)/shard_map/slice | solution.py:327
  2.4 1.3 %collective-permute-start.1 = (bf16[2,32,1,4,1024]{4,3,2,1,0:T(4,128)(2,1)S(1)}, bf16[2,32,1,4,1024]{4,3,2,1,0:T(4,128)(2,1)S(1)}, u32[]{:S(2)}, u32[]{:S(2)}) collective-permute-start(bf16[2,32,1,4,1024]{4,3,2,1,0:T(4,128)(2,1)S(1)} %get-tuple-element.22), channel_id=1, source_target_pairs={{1,0},{2,1},{3,2},{4,3},{5,4},{6,5},{7,6},{8,7},{9,8},{10,9},{11,1... | collective-permute-start | bytes 1572872 | tf_op jit(solution)/shard_map/ppermute | solution.py:327
  3.7 3.1 %collective-permute-start = (bf16[2,32,1,4,1024]{4,3,2,1,0:T(4,128)(2,1)S(1)}, bf16[2,32,1,4,1024]{4,3,2,1,0:T(4,128)(2,1)S(1)}, u32[]{:S(2)}, u32[]{:S(2)}) collective-permute-start(bf16[2,32,1,4,1024]{4,3,2,1,0:T(4,128)(2,1)S(1)} %get-tuple-element.23), channel_id=1, source_target_pairs={{0,1},{1,2},{2,3},{3,4},{4,5},{5,6},{6,7},{7,8},{8,9},{9,10},{10,1... | collective-permute-start | bytes 1572872 | tf_op jit(solution)/shard_map/ppermute | solution.py:326
  6.8 0.0 copy-done.1
  6.8 0.8 %copy.8 = bf16[3,3,3,32,32]{4,3,2,1,0:T(8,128)(2,1)} copy(bf16[3,3,3,32,32]{3,4,2,1,0:T(8,128)(2,1)S(1)} %bitcast.13) | data formatting | bytes 110592 | tf_op jit(solution)/shard_map/transpose | solution.py:334
  7.6 6.0 %weights.1 = (bf16[3,256,512]{2,1,0:T(8,128)(2,1)}, bf16[3,256,512]{2,1,0:T(8,128)(2,1)}, f32[128,128]{1,0:T(8,128)}) custom-call(bf16[27,32,32]{2,1,0:T(8,128)(2,1)} %bitcast.12, bf16[27,32,32]{2,1,0:T(8,128)(2,1)} %bitcast.14, f32[1,32]{1,0:T(1,128)} %bitcast.16), custom_call_target="tpu_custom_call" | custom-call | flops 1073741824 | bytes 4194304 | tf_op jit(solution)/shard_map/weights/pallas_call | solution.py:198
  13.6 0.0 collective-permute-done.1.hi_ref
  13.6 0.0 copy-start.3
  13.6 0.0 collective-permute-done.lo_ref
  13.7 0.0 copy-start.5
  13.7 0.8 %copy-done.3 = bf16[2,32,1,4,1024]{4,3,2,1,0:T(4,128)(2,1)} copy-done((bf16[2,32,1,4,1024]{4,3,2,1,0:T(4,128)(2,1)}, bf16[2,32,1,4,1024]{4,3,2,1,0:T(4,128)(2,1)S(1)}, u32[]{:S(2)}) %copy-start.3) | copy-done | bytes 524312
  14.5 0.2 copy-done.5
  14.7 10.0 %forward.1 = (bf16[2,32,4,4,1024]{4,3,2,1,0:T(4,128)(2,1)}, bf16[2,4,128,1024]{3,2,1,0:T(8,128)(2,1)}, bf16[2,6,128,1024]{3,2,1,0:T(8,128)(2,1)}) custom-call(bf16[2,32,4,4,1024]{4,3,2,1,0:T(4,128)(2,1)} %act_ref.1, bf16[2,32,1,4,1024]{4,3,2,1,0:T(4,128)(2,1)} %copy-done.5, bf16[2,32,1,4,1024]{4,3,2,1,0:T(4,128)(2,1)} %copy-done.3, ...), custom_call_target="tpu_custom_call" | custom-call | flops 3221225472 | bytes 10485760 | tf_op jit(solution)/shard_map/forward/pallas_call | solution.py:209
  24.6 1.3 %fusion = (bf16[2,1,128,1024]{3,2,1,0:T(8,128)(2,1)S(1)}, bf16[2,1,128,1024]{3,2,1,0:T(8,128)(2,1)S(1)}) fusion(bf16[2,4,128,1024]{3,2,1,0:T(8,128)(2,1)} %get-tuple-element.15.delta_ref), kind=kLoop, calls=%fused_computation | loop fusion | bytes 2097152 | tf_op jit(solution)/shard_map/slice | solution.py:327
  25.9 1.3 %collective-permute-start.3 = (bf16[2,1,128,1024]{3,2,1,0:T(8,128)(2,1)S(1)}, bf16[2,1,128,1024]{3,2,1,0:T(8,128)(2,1)S(1)}, u32[]{:S(2)}, u32[]{:S(2)}) collective-permute-start(bf16[2,1,128,1024]{3,2,1,0:T(8,128)(2,1)S(1)} %get-tuple-element.20), channel_id=1, source_target_pairs={{1,0},{2,1},{3,2},{4,3},{5,4},{6,5},{7,6},{8,7},{9,8},{10,9},{11,1... | collective-permute-start | bytes 1572872 | tf_op jit(solution)/shard_map/ppermute | solution.py:327
  27.2 8.8 %collective-permute-start.2 = (bf16[2,1,128,1024]{3,2,1,0:T(8,128)(2,1)S(1)}, bf16[2,1,128,1024]{3,2,1,0:T(8,128)(2,1)S(1)}, u32[]{:S(2)}, u32[]{:S(2)}) collective-permute-start(bf16[2,1,128,1024]{3,2,1,0:T(8,128)(2,1)S(1)} %get-tuple-element.21), channel_id=1, source_target_pairs={{0,1},{1,2},{2,3},{3,4},{4,5},{5,6},{6,7},{7,8},{8,9},{9,10},{10,1... | collective-permute-start | bytes 1572872 | tf_op jit(solution)/shard_map/ppermute | solution.py:326
  35.9 9.9 %weight_grad.1 = f32[256,128]{1,0:T(8,128)} custom-call(bf16[2,6,128,1024]{3,2,1,0:T(8,128)(2,1)} %get-tuple-element.17.planes_ref, bf16[2,4,128,1024]{3,2,1,0:T(8,128)(2,1)} %get-tuple-element.15.delta_ref), custom_call_target="tpu_custom_call" | custom-call | flops 3221225472 | bytes 10485760 | tf_op jit(solution)/shard_map/weight_grad/pallas_call | solution.py:290
  45.8 17.1 %all_sum.1 = (f32[27,32,32]{2,1,0:T(8,128)}, f32[1,32]{1,0:T(1,128)}) custom-call(f32[16,16,128]{2,1,0:T(8,128)} %bitcast.15), custom_call_target="tpu_custom_call" | custom-call | flops 1048576 | bytes 16777216 | tf_op jit(solution)/shard_map/all_sum/pallas_call | solution.py:274
  63.0 0.0 collective-permute-done.3.hi_ref
  63.0 0.0 copy-start.2
  63.0 0.0 collective-permute-done.2.lo_ref
  63.0 0.0 copy-start.4
  63.0 0.8 %copy-done.2 = bf16[2,1,128,1024]{3,2,1,0:T(8,128)(2,1)} copy-done((bf16[2,1,128,1024]{3,2,1,0:T(8,128)(2,1)}, bf16[2,1,128,1024]{3,2,1,0:T(8,128)(2,1)S(1)}, u32[]{:S(2)}) %copy-start.2) | copy-done | bytes 524312
  63.8 0.2 copy-done.4
  64.0 0.0 copy-start
  64.0 0.0 copy-start.6
  64.0 6.4 %input_grad.1 = bf16[2,32,4,4,1024]{4,3,2,1,0:T(4,128)(2,1)} custom-call(bf16[2,4,128,1024]{3,2,1,0:T(8,128)(2,1)} %get-tuple-element.15.delta_ref, bf16[2,1,128,1024]{3,2,1,0:T(8,128)(2,1)} %copy-done.4, bf16[2,1,128,1024]{3,2,1,0:T(8,128)(2,1)} %copy-done.2, bf16[3,256,512]{2,1,0:T(8,128)(2,1)} %get-tuple-element.16.w_ref), custom_call_target="tpu_custom_call" | custom-call | flops 3221225472 | bytes 10485760 | tf_op jit(solution)/shard_map/input_grad/pallas_call | solution.py:308
  70.3 0.0 copy-done
  70.3 0.8 %copy.11 = f32[32,32,3,3,3]{1,0,4,3,2:T(8,128)} copy(f32[32,32,3,3,3]{1,0,4,3,2:T(8,128)S(1)} %bitcast.11) | data formatting | bytes 221184
  71.1 0.0 copy-done.6
  71.1 0.5 copy.12
Async XLA Ops:
  0.6 6.1 %copy-start.1 = (bf16[32,32,3,3,3]{1,0,4,3,2:T(8,128)(2,1)S(1)}, bf16[32,32,3,3,3]{1,0,4,3,2:T(8,128)(2,1)}, u32[]{:S(2)}) copy-start(bf16[32,32,3,3,3]{1,0,4,3,2:T(8,128)(2,1)} %param.6) | copy-start | bytes 165892
  2.4 11.2 %collective-permute-start.1 = (bf16[2,32,1,4,1024]{4,3,2,1,0:T(4,128)(2,1)S(1)}, bf16[2,32,1,4,1024]{4,3,2,1,0:T(4,128)(2,1)S(1)}, u32[]{:S(2)}, u32[]{:S(2)}) collective-permute-start(bf16[2,32,1,4,1024]{4,3,2,1,0:T(4,128)(2,1)S(1)} %get-tuple-element.22), channel_id=1, source_target_pairs={{1,0},{2,1},{3,2},{4,3},{5,4},{6,5},{7,6},{8,7},{9,8},{10,9},{11,1... | collective-permute-start | bytes 1572872 | tf_op jit(solution)/shard_map/ppermute | solution.py:327
  3.7 10.0 %collective-permute-start = (bf16[2,32,1,4,1024]{4,3,2,1,0:T(4,128)(2,1)S(1)}, bf16[2,32,1,4,1024]{4,3,2,1,0:T(4,128)(2,1)S(1)}, u32[]{:S(2)}, u32[]{:S(2)}) collective-permute-start(bf16[2,32,1,4,1024]{4,3,2,1,0:T(4,128)(2,1)S(1)} %get-tuple-element.23), channel_id=1, source_target_pairs={{0,1},{1,2},{2,3},{3,4},{4,5},{5,6},{6,7},{7,8},{8,9},{9,10},{10,1... | collective-permute-start | bytes 1572872 | tf_op jit(solution)/shard_map/ppermute | solution.py:326
  13.6 0.8 %copy-start.3 = (bf16[2,32,1,4,1024]{4,3,2,1,0:T(4,128)(2,1)}, bf16[2,32,1,4,1024]{4,3,2,1,0:T(4,128)(2,1)S(1)}, u32[]{:S(2)}) copy-start(bf16[2,32,1,4,1024]{4,3,2,1,0:T(4,128)(2,1)S(1)} %collective-permute-done.1.hi_ref) | copy-start | bytes 1572868
  13.7 1.0 %copy-start.5 = (bf16[2,32,1,4,1024]{4,3,2,1,0:T(4,128)(2,1)}, bf16[2,32,1,4,1024]{4,3,2,1,0:T(4,128)(2,1)S(1)}, u32[]{:S(2)}) copy-start(bf16[2,32,1,4,1024]{4,3,2,1,0:T(4,128)(2,1)S(1)} %collective-permute-done.lo_ref) | copy-start | bytes 1572868
  25.9 37.1 %collective-permute-start.3 = (bf16[2,1,128,1024]{3,2,1,0:T(8,128)(2,1)S(1)}, bf16[2,1,128,1024]{3,2,1,0:T(8,128)(2,1)S(1)}, u32[]{:S(2)}, u32[]{:S(2)}) collective-permute-start(bf16[2,1,128,1024]{3,2,1,0:T(8,128)(2,1)S(1)} %get-tuple-element.20), channel_id=1, source_target_pairs={{1,0},{2,1},{3,2},{4,3},{5,4},{6,5},{7,6},{8,7},{9,8},{10,9},{11,1... | collective-permute-start | bytes 1572872 | tf_op jit(solution)/shard_map/ppermute | solution.py:327
  27.2 35.8 %collective-permute-start.2 = (bf16[2,1,128,1024]{3,2,1,0:T(8,128)(2,1)S(1)}, bf16[2,1,128,1024]{3,2,1,0:T(8,128)(2,1)S(1)}, u32[]{:S(2)}, u32[]{:S(2)}) collective-permute-start(bf16[2,1,128,1024]{3,2,1,0:T(8,128)(2,1)S(1)} %get-tuple-element.21), channel_id=1, source_target_pairs={{0,1},{1,2},{2,3},{3,4},{4,5},{5,6},{6,7},{7,8},{8,9},{9,10},{10,1... | collective-permute-start | bytes 1572872 | tf_op jit(solution)/shard_map/ppermute | solution.py:326
  63.0 0.8 %copy-start.2 = (bf16[2,1,128,1024]{3,2,1,0:T(8,128)(2,1)}, bf16[2,1,128,1024]{3,2,1,0:T(8,128)(2,1)S(1)}, u32[]{:S(2)}) copy-start(bf16[2,1,128,1024]{3,2,1,0:T(8,128)(2,1)S(1)} %collective-permute-done.3.hi_ref) | copy-start | bytes 1572868
  63.0 1.0 %copy-start.4 = (bf16[2,1,128,1024]{3,2,1,0:T(8,128)(2,1)}, bf16[2,1,128,1024]{3,2,1,0:T(8,128)(2,1)S(1)}, u32[]{:S(2)}) copy-start(bf16[2,1,128,1024]{3,2,1,0:T(8,128)(2,1)S(1)} %collective-permute-done.2.lo_ref) | copy-start | bytes 1572868
  64.0 6.4 %copy-start = (f32[27,32,32]{2,1,0:T(8,128)S(1)}, f32[27,32,32]{2,1,0:T(8,128)}, u32[]{:S(2)}) copy-start(f32[27,32,32]{2,1,0:T(8,128)} %get-tuple-element.18) | copy-start | bytes 331780
  64.0 7.1 %copy-start.6 = (f32[1,32]{1,0:T(1,128)S(1)}, f32[1,32]{1,0:T(1,128)}, u32[]{:S(2)}) copy-start(f32[1,32]{1,0:T(1,128)} %get-tuple-element.19) | copy-start | bytes 388
